TPU v7x, 512 devices: a whole 4x8x8 slice. The times are simulated.
512 devices in a mesh: bucket: 32 (over x, z), entity: 16 (over y, core).
Axes of the slice: x: 4, y: 8, z: 8, core: 2. Of those that a mesh axis runs over, the one named last changes fastest.
Arguments:
- ent_table: bfloat16 [16384, 512], P('entity'), may hold values from -0.25 to 0.25
- panels: bfloat16 [512, 512, 512], P(('bucket', 'entity')), may hold values from -0.25 to 0.25
- rel_vecs: bfloat16 [512, 512], P(('bucket', 'entity')), may hold values from -0.19921875 to 0.19921875
- head_slots: int32 [512, 2, 128], P(('bucket', 'entity')), may hold values from 0 to 255
- tail_slots: int32 [512, 2, 128], P(('bucket', 'entity')), may hold values from 0 to 255
- negatives: int32 [512, 2, 512], P(('bucket', 'entity')), may hold values from 0 to 255
- requests: int32 [512, 16, 16], P(('bucket', 'entity')), may hold values from 0 to 1023, as said below
- block_count: int32 [512], P(('bucket', 'entity')), may hold values from 1 to 2, as said below
Outputs:
- ent_grad: float32 [16384, 512], P('entity', 'bucket')
- panel_grad: float32 [512, 512, 512], P(('bucket', 'entity'))
- rel_grad: float32 [512, 512], P(('bucket', 'entity'))
Inputs may be any that keep to these rules, and one draw needn't show every extreme that they name: `requests`: for each device and row shard the 16 row numbers are distinct. `block_count`: at least one device has exactly 2 live blocks.
All inputs are finite; a program needn't handle non-finite values.
Results may differ from a plain program's by a relative error of at most 0.0095.
Values may be sent and summed in bfloat16 or wider, within the bound.
A program may use at most 64 MiB of HBM per device.

v0:
```python
import jax
import jax.numpy as jnp
from jax import lax
from jax.sharding import PartitionSpec as P

NEG = 512


MARGIN = 2.0


def block_terms(projected, grad_start, relation, head_one, tail_one, cand_one, live_mask):
    feature_count = projected.shape[1]
    head_rows = jnp.take(projected, head_one, axis=0)
    tail_rows = jnp.take(projected, tail_one, axis=0)
    cand_rows = jnp.take(projected, cand_one, axis=0)
    centers = (head_rows.astype(jnp.float32) + relation).astype(jnp.bfloat16)
    center_f = centers.astype(jnp.float32)
    offset = center_f - tail_rows.astype(jnp.float32)
    pos_dist = jnp.sum(offset * offset, -1)
    pos_weight = jax.nn.sigmoid(pos_dist - MARGIN) * live_mask[:, None]
    cross_terms = jnp.einsum("bed,bnd->ben", centers, cand_rows, preferred_element_type=jnp.float32)
    cand_square = jnp.sum(jnp.square(cand_rows.astype(jnp.float32)), -1)
    neg_dist = (
        jnp.sum(center_f * center_f, -1)[:, :, None] + cand_square[:, None, :] - 2.0 * cross_terms
    )
    neg_weight = -jax.nn.sigmoid(MARGIN - neg_dist) / NEG * live_mask[:, None, None]
    weight_b = neg_weight.astype(jnp.bfloat16)
    grad_center = (
        2.0 * pos_weight[..., None] * offset
        + 2.0 * jnp.sum(neg_weight, -1)[..., None] * center_f
        - 2.0 * jnp.einsum("ben,bnd->bed", weight_b, cand_rows, preferred_element_type=jnp.float32)
    )
    grad_tail = -2.0 * pos_weight[..., None] * offset
    grad_cand = 2.0 * jnp.sum(neg_weight, 1)[..., None] * cand_rows.astype(
        jnp.float32
    ) - 2.0 * jnp.einsum("ben,bed->bnd", weight_b, centers, preferred_element_type=jnp.float32)
    grad_proj = grad_start.at[head_one.reshape(-1)].add(grad_center.reshape(-1, feature_count))
    grad_proj = grad_proj.at[tail_one.reshape(-1)].add(grad_tail.reshape(-1, feature_count))
    grad_proj = grad_proj.at[cand_one.reshape(-1)].add(grad_cand.reshape(-1, feature_count))
    return (grad_proj, jnp.sum(grad_center, (0, 1)))


def body(ent_table, panels, rel_vecs, head_slots, tail_slots, negatives, requests, block_count):
    shard_count = lax.axis_size("entity")
    feature_count = ent_table.shape[1]
    asked = lax.all_to_all(requests[0], "entity", split_axis=0, concat_axis=0, tiled=True)
    found = jnp.take(ent_table, asked, axis=0)
    returned = lax.all_to_all(found, "entity", split_axis=0, concat_axis=0, tiled=True)
    fetched = returned
    fetched = fetched.reshape(-1, feature_count)
    rel_panel = panels[0]
    projected = jnp.dot(fetched, rel_panel.T, preferred_element_type=jnp.float32).astype(
        jnp.bfloat16
    )
    relation = rel_vecs[0].astype(jnp.float32)
    slot_total = head_slots.shape[1]
    grad_empty = jnp.zeros(projected.shape, jnp.float32)
    live_mask = (jnp.arange(slot_total) < block_count[0]).astype(jnp.float32)
    grad_proj, grad_rel = block_terms(
        projected, grad_empty, relation, head_slots[0], tail_slots[0], negatives[0], live_mask
    )
    grad_proj_b = grad_proj.astype(jnp.bfloat16)
    grad_fetched = jnp.dot(grad_proj_b, rel_panel, preferred_element_type=jnp.float32)
    grad_panel = jnp.einsum("kd,ke->de", grad_proj_b, fetched, preferred_element_type=jnp.float32)
    shard_rows = ent_table.shape[0]
    cap_rows = asked.shape[1]
    outgoing = grad_fetched.reshape(shard_count, cap_rows, feature_count)
    incoming = lax.all_to_all(outgoing, "entity", split_axis=0, concat_axis=0, tiled=True)
    shard_grad = jnp.zeros((shard_rows, feature_count), jnp.float32)
    shard_grad = shard_grad.at[asked.reshape(-1)].add(incoming.reshape(-1, feature_count))
    ent_part = lax.psum_scatter(shard_grad, "bucket", scatter_dimension=1, tiled=True)
    return (ent_part, grad_panel[None], grad_rel[None])


def solution(mesh):
    placed = (
        P("entity", None),
        P(("bucket", "entity"), None, None),
        P(("bucket", "entity"), None),
        P(("bucket", "entity"), None, None),
        P(("bucket", "entity"), None, None),
        P(("bucket", "entity"), None, None),
        P(("bucket", "entity"), None, None),
        P(("bucket", "entity")),
    )
    return jax.shard_map(
        body,
        mesh=mesh,
        in_specs=placed,
        out_specs=(
            P("entity", "bucket"),
            P(("bucket", "entity"), None, None),
            P(("bucket", "entity"), None),
        ),
        check_vma=False,
    )
```

profile of v0, /device:TPU:6, one launch (start us, length us, event | category | flops | bytes accessed | tf_op | source)
XLA Modules:
  0.0 323.0 jit_solution(11476167738534634844)
XLA Ops:
  7.2 0.0 copy-start
  7.2 0.0 copy-start.6
  7.2 0.0 copy-start.3
  7.2 7.3 %all-to-all-start = ((s32[16,1,16]{2,1,0:T(1,128)}), s32[16,1,16]{2,1,0:T(1,128)S(1)}, u32[]{:S(2)}, u32[]{:S(2)}) async-start(s32[16,1,16]{2,1,0:T(1,128)} %bitcast.104), calls=%async_computation | async-start | bytes 16384 | tf_op jit(solution)/shard_map/all_to_all | solution.py:47
  14.6 0.7 fusion.27
  15.3 0.7 compare_and_fusion
  16.0 0.7 fusion.28
  16.6 0.7 compare_and_fusion.2
  17.3 0.7 fusion.29
  18.0 0.7 compare_select_fusion.6
  19.4 0.7 compare_select_fusion.5
  20.1 2.0 all-to-all-done
  22.1 0.1 reshape.309
  22.2 1.2 gather_fusion
  23.3 0.8 broadcast_select_fusion.4
  24.1 5.2 %all-to-all-start.1 = ((bf16[16,16,512]{2,1,0:T(8,128)(2,1)}), bf16[16,16,512]{2,1,0:T(8,128)(2,1)S(1)}, u32[]{:S(2)}, u32[]{:S(2)}) async-start(bf16[16,16,512]{2,1,0:T(8,128)(2,1)} %broadcast_select_fusion.4), calls=%async_computation.1 | async-start | bytes 524288 | tf_op jit(solution)/shard_map/all_to_all | solution.py:49
  29.5 11.1 %all-to-all-done.1 = bf16[16,16,512]{2,1,0:T(8,128)(2,1)S(1)} async-done(((bf16[16,16,512]{2,1,0:T(8,128)(2,1)}), bf16[16,16,512]{2,1,0:T(8,128)(2,1)S(1)}, u32[]{:S(2)}, u32[]{:S(2)}) %all-to-all-start.1) | async-done | bytes 262176 | tf_op jit(solution)/shard_map/all_to_all | solution.py:49
  40.6 0.7 copy-done.1
  41.3 0.3 convolution_convert_fusion
  41.6 4.0 %gather_fusion.1 = bf16[1024,512]{1,0:T(8,128)(2,1)S(1)} fusion(bf16[256,512]{1,0:T(8,128)(2,1)S(1)} %convolution_convert_fusion, s32[1024]{0:T(1024)S(1)} %broadcast_clamp_fusion), kind=kCustom, calls=%fused_computation.3 | custom fusion | bytes 2101248 | tf_op jit(solution)/shard_map/jit(_take)/gather | solution.py:16
  45.6 1.2 gather_fusion.2
  46.8 0.5 fusion.1
  47.3 0.4 fusion.12
  47.7 0.7 fusion.32
  48.4 1.2 gather_fusion.3
  49.6 0.3 multiply_reduce_fusion
  49.8 0.1 broadcast_multiply_fusion.3
  49.9 0.2 fusion.22
  50.1 2.0 fusion.2
  52.2 1.9 fusion.33
  54.0 2.7 scatter_custom_fusion
  56.7 2.3 scatter_fusion
  59.1 0.0 copy-start.4
  59.1 7.5 %scatter_fusion.1 = f32[256,512]{1,0:T(8,128)S(1)} fusion(f32[256,512]{1,0:T(8,128)S(1)} %scatter_fusion, s32[1024]{0:T(1024)S(1)} %bitcast.99, f32[1024,512]{1,0:T(8,128)} %bitcast.86), kind=kCustom, calls=%fused_computation.6 | custom fusion | flops 524288 | bytes 6295552 | tf_op jit(solution)/shard_map/scatter-add | solution.py:40
  66.6 1.1 fusion.17
  67.7 3.6 %all-to-all-start.2 = ((f32[16,16,512]{2,1,0:T(8,128)}), f32[16,16,512]{2,1,0:T(8,128)S(1)}, u32[]{:S(2)}, u32[]{:S(2)}) async-start(f32[16,16,512]{2,1,0:T(8,128)} %fusion.17), calls=%async_computation.2 | async-start | bytes 1048576 | tf_op jit(solution)/shard_map/all_to_all | solution.py:69
  71.3 0.2 reduce-scatter.4.cloned.1.call-start
  71.5 0.5 broadcast.247
  72.1 0.7 reduce.3
  72.7 0.1 reshape.284
  72.8 14.6 %all-to-all-done.2 = f32[16,16,512]{2,1,0:T(8,128)S(1)} async-done(((f32[16,16,512]{2,1,0:T(8,128)}), f32[16,16,512]{2,1,0:T(8,128)S(1)}, u32[]{:S(2)}, u32[]{:S(2)}) %all-to-all-start.2) | async-done | bytes 524320 | tf_op jit(solution)/shard_map/all_to_all | solution.py:69
  87.4 0.8 copy-done.5
  88.2 3.1 scatter_custom_fusion.3
  91.3 1.9 copy.18
  93.2 0.0 reduce-scatter.4.cloned.1.call-update
  93.2 0.9 copy-done.2
  94.1 1.3 convolution_bitcast_fusion
  95.4 220.7 %reduce-scatter.4.cloned.1.call-done = f32[16,1024]{1,0:T(8,128)} async-done(((f32[512,1024]{1,0:T(8,128)}), f32[16,1024]{1,0:T(8,128)}) %reduce-scatter.4.cloned.1.call-update) | async-done | bytes 65552
  (26 shorter events, 0.1 us)
Async XLA Ops:
  7.2 15.0 %copy-start = (bf16[1024,512]{1,0:T(8,128)(2,1)S(1)}, bf16[1024,512]{1,0:T(8,128)(2,1)}, u32[]{:S(2)}) copy-start(bf16[1024,512]{1,0:T(8,128)(2,1)} %param.10) | copy-start | bytes 3145732
  7.2 22.3 %copy-start.6 = (s32[1,2,512]{2,1,0:T(2,128)S(1)}, s32[1,2,512]{2,1,0:T(2,128)}, u32[]{:S(2)}) copy-start(s32[1,2,512]{2,1,0:T(2,128)} %param.15) | copy-start | bytes 12292
  7.2 22.2 %copy-start.7 = (bf16[1,512]{1,0:T(2,128)(2,1)S(1)}, bf16[1,512]{1,0:T(2,128)(2,1)}, u32[]{:S(2)}) copy-start(bf16[1,512]{1,0:T(2,128)(2,1)} %param.12) | copy-start | bytes 3076
  7.2 34.1 %copy-start.3 = (bf16[1,512,512]{2,1,0:T(8,128)(2,1)S(1)}, bf16[1,512,512]{2,1,0:T(8,128)(2,1)}, u32[]{:S(2)}) copy-start(bf16[1,512,512]{2,1,0:T(8,128)(2,1)} %param.11) | copy-start | bytes 1572868
  7.2 14.9 %all-to-all-start = ((s32[16,1,16]{2,1,0:T(1,128)}), s32[16,1,16]{2,1,0:T(1,128)S(1)}, u32[]{:S(2)}, u32[]{:S(2)}) async-start(s32[16,1,16]{2,1,0:T(1,128)} %bitcast.104), calls=%async_computation | async-start | bytes 16384 | tf_op jit(solution)/shard_map/all_to_all | solution.py:47
  24.1 16.4 %all-to-all-start.1 = ((bf16[16,16,512]{2,1,0:T(8,128)(2,1)}), bf16[16,16,512]{2,1,0:T(8,128)(2,1)S(1)}, u32[]{:S(2)}, u32[]{:S(2)}) async-start(bf16[16,16,512]{2,1,0:T(8,128)(2,1)} %broadcast_select_fusion.4), calls=%async_computation.1 | async-start | bytes 524288 | tf_op jit(solution)/shard_map/all_to_all | solution.py:49
  40.6 0.7 copy-start.1
  59.1 7.6 %copy-start.4 = (bf16[1,512,512]{2,1,0:T(8,128)(2,1)S(1)}, bf16[1,512,512]{2,1,0:T(8,128)(2,1)}, u32[]{:S(2)}) copy-start(bf16[1,512,512]{2,1,0:T(8,128)(2,1)} %param.11) | copy-start | bytes 1572868
  67.7 19.6 %all-to-all-start.2 = ((f32[16,16,512]{2,1,0:T(8,128)}), f32[16,16,512]{2,1,0:T(8,128)S(1)}, u32[]{:S(2)}, u32[]{:S(2)}) async-start(f32[16,16,512]{2,1,0:T(8,128)} %fusion.17), calls=%async_computation.2 | async-start | bytes 1048576 | tf_op jit(solution)/shard_map/all_to_all | solution.py:69
  71.3 244.8 %reduce-scatter.4.cloned.1.call-start = ((), (), s32[]{:S(2)}) async-start(), calls=%async_computation.4 | async-start | bytes 2162688
  87.4 0.8 copy-start.5
  93.1 0.9 copy-start.2
Sparse Core Ops, SparseCore 0:
  93.3 222.7 reduce-scatter.3
where the time goes:
time: 324 us; the launch traced here: 323 us
  waiting for transfers between devices  248 us (77%)
  other arithmetic  23.5 us (7%)
  starting transfers between devices  16.4 us (5%)
  between operations  14.9 us (5%)
  local copies, waits for them, and re-layouts  12.5 us (4%)
  matrix products  7.32 us (2%)
    unnamed x2, waiting for transfers between devices  221 us
    all_to_all x1, waiting for transfers between devices, body(): lax.all_to_all(outgoing, 'entity', split_axis=0, concat_axis=0, tiled=True)  14.6 us
    all_to_all x1, waiting for transfers between devices, body(): lax.all_to_all(found, 'entity', split_axis=0, concat_axis=0, tiled=True)  11.1 us
    scatter-add x1, other arithmetic, block_terms(): grad_proj.at[cand_one.reshape(-1)].add(grad_cand.reshape(-1, feature_count))  7.51 us
    all_to_all x1, starting transfers between devices, body(): lax.all_to_all(requests[0], 'entity', split_axis=0, concat_axis=0, tiled=...  7.35 us
  transfers between devices with their start and end apart: 4, of which 4 were waited for; matrix products, arithmetic and copies ran while one was open for 2% of the time, Pallas kernels for 0%

commit v1 on v0

v1 whole, which is shorter than its diff:
```python
import functools

import jax
import jax.numpy as jnp
from jax import lax
from jax.experimental import pallas as pl
from jax.experimental.pallas import tpu as pltpu
from jax.sharding import PartitionSpec as P

MARGIN = 2.0
LANES = 128
MESH = pl.DeviceIdType.MESH
BF = jnp.bfloat16
F32 = jnp.float32


def mm(a, b):
    return jnp.dot(a, b, preferred_element_type=F32)


def mm_nt(a, b):
    return lax.dot_general(a, b, (((1,), (1,)), ((), ())), preferred_element_type=F32)


def iota(shape, axis):
    return lax.broadcasted_iota(jnp.int32, shape, axis)


def to_col(row):
    n = row.shape[1]
    eye = iota((n, n), 0) == iota((n, n), 1)
    return jnp.sum(jnp.where(eye, row, 0.0), axis=1, keepdims=True)


def to_row(col):
    n = col.shape[0]
    eye = iota((n, n), 0) == iota((n, n), 1)
    return jnp.sum(jnp.where(eye, col, 0.0), axis=0, keepdims=True)


def one_hot(row, n):
    return (iota((n, row.shape[1]), 0) == row).astype(F32)


def local_terms(fetched, panel, rel, head_ref, tail_ref, neg_ref, live_count):
    blocks, edge = head_ref.shape
    neg = neg_ref.shape[1]
    slots = fetched.shape[0]
    edges = blocks * edge
    proj = mm_nt(fetched, panel).astype(BF)
    proj_f = proj.astype(F32)
    head = jnp.concatenate([head_ref[j : j + 1, :] for j in range(blocks)], axis=1)
    tail = jnp.concatenate([tail_ref[j : j + 1, :] for j in range(blocks)], axis=1)
    head_t = one_hot(head, slots)
    tail_t = one_hot(tail, slots)
    block_of = iota((edges, 1), 0) // edge
    live = (block_of < live_count).astype(F32)
    count = jnp.zeros((edges, slots), F32)
    for j in range(blocks):
        hits = jnp.sum(one_hot(neg_ref[j : j + 1, :], slots), axis=1, keepdims=True)
        count = jnp.where(block_of == j, to_row(hits), count)

    centers = (mm(head_t.T.astype(BF), proj) + rel).astype(BF)
    center_f = centers.astype(F32)
    offset = center_f - mm(tail_t.T.astype(BF), proj)
    pos_weight = jax.nn.sigmoid(jnp.sum(offset * offset, axis=1, keepdims=True) - MARGIN) * live
    proj_sq = to_row(jnp.sum(proj_f * proj_f, axis=1, keepdims=True))
    center_sq = jnp.sum(center_f * center_f, axis=1, keepdims=True)
    dist = center_sq + proj_sq - 2.0 * mm_nt(centers, proj)
    weight = -jax.nn.sigmoid(MARGIN - dist) * (live * (1.0 / neg)) * count
    weight_t = weight.T
    pulled = 2.0 * pos_weight * offset
    grad_center = (
        pulled
        + 2.0 * jnp.sum(weight, axis=1, keepdims=True) * center_f
        - 2.0 * mm(weight.astype(BF), proj)
    )
    grad_proj = (
        mm(head_t.astype(BF), grad_center.astype(BF))
        - mm(tail_t.astype(BF), pulled.astype(BF))
        + 2.0 * jnp.sum(weight_t, axis=1, keepdims=True) * proj_f
        - 2.0 * mm(weight_t.astype(BF), centers)
    ).astype(BF)
    return grad_proj, jnp.sum(grad_center, axis=0, keepdims=True)


def kernel(
    nb, ne,
    table_hbm, panel_hbm, rel_ref, head_ref, tail_ref, neg_ref, req_ref, count_ref,
    ent_ref, proj_out, fetched_out, rel_out,
    table, panel, msg, reqbuf, asked_all, rows, fetched, gf, grecv, gt, frecv, spread, hot,
    lsem, qs, qr, as_, ar, cs, cr, es, er, fs, fr,
):
    b = lax.axis_index("bucket")
    e = lax.axis_index("entity")
    cap = req_ref.shape[1]
    slots = ne * cap
    width = frecv.shape[2]
    halves = frecv.shape[1]
    per_half = ne // halves
    table_rows = table.shape[0]

    load_table = pltpu.make_async_copy(table_hbm, table, lsem.at[0])
    load_panel = pltpu.make_async_copy(panel_hbm, panel, lsem.at[1])
    load_table.start()
    load_panel.start()

    def entity_peer(j):
        return lax.rem(e + j, ne)

    def bucket_peer(i):
        return lax.rem(b + i, nb)

    def each(lo, hi, do):
        def step(k, carry):
            do(k)
            return carry

        lax.fori_loop(lo, hi, step, 0)

    barrier = pltpu.get_barrier_semaphore()
    each(1, ne, lambda j: pl.semaphore_signal(
        barrier, inc=1, device_id={"entity": entity_peer(j)}, device_id_type=MESH))
    each(1, nb, lambda i: pl.semaphore_signal(
        barrier, inc=1, device_id={"bucket": bucket_peer(i)}, device_id_type=MESH))

    req = req_ref[...]
    repeat = (iota((cap, slots), 0) == lax.rem(iota((cap, slots), 1), cap)).astype(BF)
    high = mm((req >> 5).astype(F32).astype(BF), repeat)
    low = mm((req & 31).astype(F32).astype(BF), repeat)
    tiled = (high * 32.0 + low).astype(jnp.int32)
    slot_of = lax.rem(iota((ne, slots), 0) - e + ne, ne)
    tiled = jnp.where(iota((ne, slots), 1) // cap == slot_of, tiled, 0)
    for o in range(ne):
        msg[o] = tiled[o : o + 1, :]

    pl.semaphore_wait(barrier, ne + nb - 2)

    def request_copy(j):
        return pltpu.make_async_remote_copy(
            src_ref=msg.at[entity_peer(j)], dst_ref=reqbuf.at[j], send_sem=qs.at[j],
            recv_sem=qr.at[j], device_id={"entity": entity_peer(j)}, device_id_type=MESH)

    each(1, ne, lambda j: request_copy(j).start())
    reqbuf[0] = msg[e]
    each(1, ne, lambda j: request_copy(j).wait())
    asked = reqbuf[0]
    for j in range(1, ne):
        asked = asked + reqbuf[j]
    asked_all[0] = asked

    def asked_copy(i):
        return pltpu.make_async_remote_copy(
            src_ref=asked_all.at[0], dst_ref=asked_all.at[i], send_sem=as_.at[i],
            recv_sem=ar.at[i], device_id={"bucket": bucket_peer(i)}, device_id_type=MESH)

    load_table.wait()
    asked_col = to_col(asked.astype(F32)).astype(jnp.int32)
    pick = (iota((slots, table_rows), 1) == asked_col).astype(F32).astype(BF)
    rows[...] = mm(pick, table[...]).astype(BF)

    def at_slot(o):
        return pl.ds(pl.multiple_of(o * cap, cap), cap)

    def row_copy(j):
        return pltpu.make_async_remote_copy(
            src_ref=rows.at[at_slot(j)], dst_ref=fetched.at[at_slot(e)], send_sem=cs.at[j],
            recv_sem=cr.at[j], device_id={"entity": lax.rem(e - j + ne, ne)}, device_id_type=MESH)

    each(1, ne, lambda j: row_copy(j).start())
    each(1, nb, lambda i: asked_copy(i).start())
    fetched[at_slot(e), :] = rows[0:cap, :]
    load_panel.wait()
    each(1, ne, lambda j: row_copy(j).wait())

    grad_proj, grad_rel = local_terms(
        fetched[...], panel[...], rel_ref[...].astype(F32), head_ref, tail_ref, neg_ref, count_ref[0])
    gf[...] = mm(grad_proj, panel[...]).astype(BF)

    def grad_copy(j):
        return pltpu.make_async_remote_copy(
            src_ref=gf.at[at_slot(entity_peer(j))], dst_ref=grecv.at[at_slot(j)],
            send_sem=es.at[j], recv_sem=er.at[j],
            device_id={"entity": entity_peer(j)}, device_id_type=MESH)

    each(1, ne, lambda j: grad_copy(j).start())
    grecv[0:cap, :] = gf[at_slot(e), :]
    rel_out[...] = grad_rel
    proj_out[...] = grad_proj
    fetched_out[...] = fetched[...]

    each(1, nb, lambda i: asked_copy(i).wait())
    for i in range(nb):
        hi = asked_all[i] & (LANES - 1)
        hot[:, i * slots : (i + 1) * slots] = one_hot(hi, LANES).astype(BF)

    def part_copy(h, i):
        return pltpu.make_async_remote_copy(
            src_ref=gt.at[h, pl.ds(pl.multiple_of(bucket_peer(i) * width, width), width), :],
            dst_ref=frecv.at[i, h], send_sem=fs.at[h, i], recv_sem=fr.at[h, i],
            device_id={"bucket": bucket_peer(i)}, device_id_type=MESH)

    for h in range(halves):
        first = h * per_half
        each(max(first, 1), first + per_half, lambda j: grad_copy(j).wait())
        piece = grecv[first * cap : (first + per_half) * cap, :].astype(F32)
        gt[h] = piece.T.astype(BF)
        each(1, nb, lambda i, h=h: part_copy(h, i).start())
        frecv[0, h] = gt[h, pl.ds(pl.multiple_of(b * width, width), width), :]

    high_rows = table_rows // LANES
    half_lanes = per_half * cap
    for i in range(nb):
        for h in range(halves):
            if i:
                part_copy(h, i).wait()
            at = i * slots + h * half_lanes
            lo = asked_all[i, :, h * half_lanes : (h + 1) * half_lanes] >> 7
            g = frecv[i, h].astype(F32)
            spread[:, at : at + half_lanes] = jnp.concatenate(
                [jnp.where(lo == k, g, 0.0) for k in range(high_rows)], axis=0).astype(BF)
    total = mm_nt(spread[...], hot[...])
    for k in range(high_rows):
        ent_ref[:, k * LANES : (k + 1) * LANES] = total[k * width : (k + 1) * width, :]


def body(ent_table, panels, rel_vecs, head_slots, tail_slots, negatives, requests, block_count):
    nb = lax.axis_size("bucket")
    ne = lax.axis_size("entity")
    rows, feat = ent_table.shape
    cap = requests.shape[2]
    slots = ne * cap
    width = feat // nb
    halves = 2
    vmem = pl.BlockSpec(memory_space=pltpu.VMEM)
    anywhere = pl.BlockSpec(memory_space=pl.ANY)
    smem = pl.BlockSpec(memory_space=pltpu.SMEM)
    dma = pltpu.SemaphoreType.DMA
    ent_t, grad_proj, fetched, grad_rel = pl.pallas_call(
        functools.partial(kernel, nb, ne),
        out_shape=(
            jax.ShapeDtypeStruct((width, rows), F32),
            jax.ShapeDtypeStruct((slots, feat), BF),
            jax.ShapeDtypeStruct((slots, feat), BF),
            jax.ShapeDtypeStruct((1, feat), F32),
        ),
        in_specs=[anywhere, anywhere, vmem, vmem, vmem, vmem, vmem, smem],
        out_specs=(vmem, vmem, vmem, vmem),
        scratch_shapes=[
            pltpu.VMEM((rows, feat), BF),
            pltpu.VMEM((feat, feat), BF),
            pltpu.VMEM((ne, 1, slots), jnp.int32),
            pltpu.VMEM((ne, 1, slots), jnp.int32),
            pltpu.VMEM((nb, 1, slots), jnp.int32),
            pltpu.VMEM((slots, feat), BF),
            pltpu.VMEM((slots, feat), BF),
            pltpu.VMEM((slots, feat), BF),
            pltpu.VMEM((slots, feat), BF),
            pltpu.VMEM((halves, feat, slots // halves), BF),
            pltpu.VMEM((nb, halves, width, slots // halves), BF),
            pltpu.VMEM((rows // LANES * width, nb * slots), BF),
            pltpu.VMEM((LANES, nb * slots), BF),
            dma((2,)),
            dma((ne,)), dma((ne,)),
            dma((nb,)), dma((nb,)),
            dma((ne,)), dma((ne,)),
            dma((ne,)), dma((ne,)),
            dma((halves, nb)), dma((halves, nb)),
        ],
        compiler_params=pltpu.CompilerParams(
            collective_id=0, has_side_effects=True, vmem_limit_bytes=48 * 1024 * 1024
        ),
        name="transr",
    )(
        ent_table, panels[0], rel_vecs, head_slots[0], tail_slots[0], negatives[0],
        requests[0], block_count,
    )
    grad_panel = jnp.einsum("kd,ke->de", grad_proj, fetched, preferred_element_type=F32)
    return (ent_t.T, grad_panel[None], grad_rel)


def solution(mesh):
    both = ("bucket", "entity")
    placed = (
        P("entity", None),
        P(both, None, None),
        P(both, None),
        P(both, None, None),
        P(both, None, None),
        P(both, None, None),
        P(both, None, None),
        P(both),
    )
    return jax.shard_map(
        body,
        mesh=mesh,
        in_specs=placed,
        out_specs=(P("entity", "bucket"), P(both, None, None), P(both, None)),
        check_vma=False,
    )
```

time: 324 us -> 61.5 us (0.19)
  waiting for transfers between devices: 248 us -> 0 us
  Pallas kernels: 0 us -> 52.5 us
  other arithmetic: 23.5 us -> 0 us
  starting transfers between devices: 16.4 us -> 0 us
  between operations: 14.9 us -> 1.33 us
  local copies, waits for them, and re-layouts: 12.5 us -> 5.52 us
  matrix products: 7.32 us -> 1.29 us
    unnamed x2 -> x0, waiting for transfers between devices: 221 us -> none
    pallas_call x0 -> x1, Pallas kernels: none -> 52.5 us  [body(): pl.pallas_call(functools.partial(kernel, nb, ne), out_shape=(jax.ShapeDty...]
    all_to_all x3 -> x0, waiting for transfers between devices: 27.6 us -> none  [the longest x1 14.6 us: body(): lax.all_to_all(outgoing, 'entity', split_axis=0, concat_axis=0, tiled=True)]
    all_to_all x3 -> x0, starting transfers between devices: 16.2 us -> none  [the longest x1 7.35 us: body(): lax.all_to_all(requests[0], 'entity', split_axis=0, concat_axis=0, tiled=...]
    scatter-add x4 -> x0, other arithmetic: 15.6 us -> none  [the longest x1 7.51 us: block_terms(): grad_proj.at[cand_one.reshape(-1)].add(grad_cand.reshape(-1, feature_count))]
    gather x4 -> x0, local copies, waits for them, and re-layouts: 7.43 us -> none  [the longest x1 3.97 us: block_terms(): cand_rows = jnp.take(projected, cand_one, axis=0)]
    dot_general x6 -> x1, matrix products: 7.32 us -> 1.29 us  [body(): jnp.einsum('kd,ke->de', grad_proj, fetched, preferred_element_type=F32)]
  transfers between devices with their start and end apart: 4 -> 0, of which waited for: 4 -> 0; matrix products, arithmetic and copies ran while one was open for 2% -> 0% of each run, Pallas kernels for 0% -> 0%
where the time goes in v1:
time: 61.5 us; the launch traced here: 60.6 us
  Pallas kernels  52.5 us (85%)
  local copies, waits for them, and re-layouts  5.52 us (9%)
  between operations  1.33 us (2%)
  matrix products  1.29 us (2%)
    pallas_call x1, Pallas kernels, body(): pl.pallas_call(functools.partial(kernel, nb, ne), out_shape=(jax.ShapeDty...  52.5 us
    unnamed x16, local copies, waits for them, and re-layouts  5.52 us
    dot_general x1, matrix products, body(): jnp.einsum('kd,ke->de', grad_proj, fetched, preferred_element_type=F32)  1.29 us

profile of v1, /device:TPU:6, one launch (start us, length us, event | category | flops | bytes accessed | tf_op | source)
XLA Modules:
  0.0 60.6 jit_solution(8345654811385631879)
XLA Ops:
  0.6 0.0 copy-start.2
  1.3 0.0 copy-start.4
  1.3 0.0 copy-start.5
  1.3 0.0 copy-done.2
  1.3 0.7 %copy-done.4 = bf16[1,512]{1,0:T(2,128)(2,1)S(1)} copy-done((bf16[1,512]{1,0:T(2,128)(2,1)S(1)}, bf16[1,512]{1,0:T(2,128)(2,1)}, u32[]{:S(2)}) %copy-start.4) | copy-done | bytes 1048
  2.0 0.0 copy-done.5
  2.0 0.0 copy-start
  2.0 1.2 %copy-done = bf16[1024,512]{1,0:T(8,128)(2,1)S(1)} copy-done((bf16[1024,512]{1,0:T(8,128)(2,1)S(1)}, bf16[1024,512]{1,0:T(8,128)(2,1)}, u32[]{:S(2)}) %copy-start) | copy-done | bytes 1048600
  3.2 0.0 copy-start.1
  3.2 1.0 %copy-done.1 = bf16[1,512,512]{2,1,0:T(8,128)(2,1)S(1)} copy-done((bf16[1,512,512]{2,1,0:T(8,128)(2,1)S(1)}, bf16[1,512,512]{2,1,0:T(8,128)(2,1)}, u32[]{:S(2)}) %copy-start.1) | copy-done | bytes 524312
  4.3 0.0 copy-start.3
  4.3 0.7 %copy-done.3 = s32[1,2,512]{2,1,0:T(2,128)S(1)} copy-done((s32[1,2,512]{2,1,0:T(2,128)S(1)}, s32[1,2,512]{2,1,0:T(2,128)}, u32[]{:S(2)}) %copy-start.3) | copy-done | bytes 4120
  5.0 0.0 copy-start.6
  5.0 0.7 %copy-done.6 = s32[1,2,128]{2,1,0:T(2,128)S(1)} copy-done((s32[1,2,128]{2,1,0:T(2,128)S(1)}, s32[1,2,128]{2,1,0:T(2,128)}, u32[]{:S(2)}) %copy-start.6) | copy-done | bytes 1048
  5.6 52.5 %transr.1 = (f32[16,1024]{1,0:T(8,128)S(1)}, bf16[256,512]{1,0:T(8,128)(2,1)S(1)}, bf16[256,512]{1,0:T(8,128)(2,1)S(1)}, f32[1,512]{1,0:T(1,128)S(1)}) custom-call(bf16[1024,512]{1,0:T(8,128)(2,1)S(1)} %copy-done, bf16[512,512]{1,0:T(8,128)(2,1)S(1)} %bitcast.10, bf16[1,512]{1,0:T(2,128)(2,1)S(1)} %copy-done.4, s32[2,128]{1,0:T(2,128)S(1)} %bitcast.14, ...), custom_call_target="tpu_custom_call" | custom-call | tf_op jit(solution)/shard_map/transr/pallas_call | solution.py:239
  58.1 1.3 %convolution_bitcast_fusion = f32[1,512,512]{2,1,0:T(8,128)} fusion(bf16[256,512]{1,0:T(8,128)(2,1)S(1)} %get-tuple-element.8, bf16[256,512]{1,0:T(8,128)(2,1)S(1)} %get-tuple-element.9), kind=kOutput, calls=%fused_computation | convolution fusion | flops 134217728 | bytes 1572864 | tf_op jit(solution)/shard_map/kd,ke->de/dot_general | solution.py:278
  59.4 0.6 %copy.14 = f32[1024,16]{0,1:T(8,128)} copy(f32[1024,16]{0,1:T(8,128)S(1)} %bitcast.11) | data formatting | bytes 131072
  60.0 0.6 copy.15
Async XLA Ops:
  0.6 0.7 %copy-start.2 = (s32[1,16,16]{2,1,0:T(8,128)S(1)}, s32[1,16,16]{2,1,0:T(8,128)}, u32[]{:S(2)}) copy-start(s32[1,16,16]{2,1,0:T(8,128)} %param.14) | copy-start | bytes 3076
  1.3 0.7 %copy-start.4 = (bf16[1,512]{1,0:T(2,128)(2,1)S(1)}, bf16[1,512]{1,0:T(2,128)(2,1)}, u32[]{:S(2)}) copy-start(bf16[1,512]{1,0:T(2,128)(2,1)} %rel_ref.1) | copy-start | bytes 3076
  1.3 0.7 %copy-start.5 = (s32[1,2,128]{2,1,0:T(2,128)S(1)}, s32[1,2,128]{2,1,0:T(2,128)}, u32[]{:S(2)}) copy-start(s32[1,2,128]{2,1,0:T(2,128)} %param.11) | copy-start | bytes 3076
  2.0 1.2 %copy-start = (bf16[1024,512]{1,0:T(8,128)(2,1)S(1)}, bf16[1024,512]{1,0:T(8,128)(2,1)}, u32[]{:S(2)}) copy-start(bf16[1024,512]{1,0:T(8,128)(2,1)} %table_hbm.1) | copy-start | bytes 3145732
  3.2 1.0 %copy-start.1 = (bf16[1,512,512]{2,1,0:T(8,128)(2,1)S(1)}, bf16[1,512,512]{2,1,0:T(8,128)(2,1)}, u32[]{:S(2)}) copy-start(bf16[1,512,512]{2,1,0:T(8,128)(2,1)} %param.9) | copy-start | bytes 1572868
  4.3 0.7 %copy-start.3 = (s32[1,2,512]{2,1,0:T(2,128)S(1)}, s32[1,2,512]{2,1,0:T(2,128)}, u32[]{:S(2)}) copy-start(s32[1,2,512]{2,1,0:T(2,128)} %param.13) | copy-start | bytes 12292
  5.0 0.7 %copy-start.6 = (s32[1,2,128]{2,1,0:T(2,128)S(1)}, s32[1,2,128]{2,1,0:T(2,128)}, u32[]{:S(2)}) copy-start(s32[1,2,128]{2,1,0:T(2,128)} %param.12) | copy-start | bytes 3076

commit v2 on v1

v2 whole, which is shorter than its diff:
```python
import functools

import jax
import jax.numpy as jnp
from jax import lax
from jax.experimental import pallas as pl
from jax.experimental.pallas import tpu as pltpu
from jax.sharding import PartitionSpec as P

MARGIN = 2.0
LANES = 128
HALVES = 2
X_SIZE = 4
MESH = pl.DeviceIdType.MESH
BF = jnp.bfloat16
F32 = jnp.float32


def mm(a, b):
    return jnp.dot(a, b, preferred_element_type=F32)


def mm_nt(a, b):
    return lax.dot_general(a, b, (((1,), (1,)), ((), ())), preferred_element_type=F32)


def mm_tn(a, b):
    return lax.dot_general(a, b, (((0,), (0,)), ((), ())), preferred_element_type=F32)


def iota(shape, axis):
    return lax.broadcasted_iota(jnp.int32, shape, axis)


def to_col(row):
    n = row.shape[1]
    eye = iota((n, n), 0) == iota((n, n), 1)
    return jnp.sum(jnp.where(eye, row, 0.0), axis=1, keepdims=True)


def to_row(col):
    n = col.shape[0]
    eye = iota((n, n), 0) == iota((n, n), 1)
    return jnp.sum(jnp.where(eye, col, 0.0), axis=0, keepdims=True)


def one_hot(row, n):
    return (iota((n, row.shape[1]), 0) == row).astype(F32)


def slot_tables(head_ref, tail_ref, neg_ref, live_count, slots):
    blocks, edge = head_ref.shape
    edges = blocks * edge
    head = jnp.concatenate([head_ref[j : j + 1, :] for j in range(blocks)], axis=1)
    tail = jnp.concatenate([tail_ref[j : j + 1, :] for j in range(blocks)], axis=1)
    head_t = one_hot(head, slots)
    tail_t = one_hot(tail, slots)
    block_of = iota((edges, 1), 0) // edge
    live = (block_of < live_count).astype(F32)
    count = jnp.zeros((edges, slots), F32)
    for j in range(blocks):
        hits = jnp.sum(one_hot(neg_ref[j : j + 1, :], slots), axis=1, keepdims=True)
        count = jnp.where(block_of == j, to_row(hits), count)
    count = count * (live * (1.0 / neg_ref.shape[1]))
    return head_t.astype(BF), tail_t.astype(BF), head_t.T.astype(BF), tail_t.T.astype(BF), live, count


def local_terms(fetched, panel, rel, tables):
    head_t, tail_t, head, tail, live, count = tables
    proj = mm_nt(fetched, panel).astype(BF)
    proj_f = proj.astype(F32)
    centers = (mm(head, proj) + rel).astype(BF)
    center_f = centers.astype(F32)
    offset = center_f - mm(tail, proj)
    pos_weight = jax.nn.sigmoid(jnp.sum(offset * offset, axis=1, keepdims=True) - MARGIN) * live
    proj_sq = to_row(jnp.sum(proj_f * proj_f, axis=1, keepdims=True))
    center_sq = jnp.sum(center_f * center_f, axis=1, keepdims=True)
    dist = center_sq + proj_sq - 2.0 * mm_nt(centers, proj)
    weight = -jax.nn.sigmoid(MARGIN - dist) * count
    weight_t = weight.T
    pulled = 2.0 * pos_weight * offset
    grad_center = (
        pulled
        + 2.0 * jnp.sum(weight, axis=1, keepdims=True) * center_f
        - 2.0 * mm(weight.astype(BF), proj)
    )
    grad_proj = (
        mm(head_t, grad_center.astype(BF))
        - mm(tail_t, pulled.astype(BF))
        + 2.0 * jnp.sum(weight_t, axis=1, keepdims=True) * proj_f
        - 2.0 * mm(weight_t.astype(BF), centers)
    ).astype(BF)
    return grad_proj, jnp.sum(grad_center, axis=0, keepdims=True)


def away(step, size):
    return min(step, size - step)


def kernel(
    nb, ne,
    table_hbm, panel_hbm, rel_hbm, head_hbm, tail_hbm, neg_hbm, req_hbm, count_ref,
    ent_ref, proj_out, fetched_out, rel_out,
    table, panel, rel_v, head_v, tail_v, neg_v, req_v, wide,
    msg, reqbuf, asked_all, rows, fetched, gf, grecv, gt, frecv, spread, hot,
    lsem, qs, qr, as_, ar, cs, cr, es, er, fs, fr,
):
    b = lax.axis_index("bucket")
    e = lax.axis_index("entity")
    cap = req_v.shape[1]
    slots = ne * cap
    width = frecv.shape[2]
    per_half = ne // HALVES
    half_lanes = per_half * cap
    table_rows = table.shape[0]
    high_rows = table_rows // LANES

    chips = ne // 2
    steps = sorted(range(chips), key=lambda d: away(d, chips))

    def ahead(s):
        return 2 * ((e // 2 + steps[s // 2]) & (chips - 1)) + ((e + s) & 1)

    def behind(s):
        return 2 * ((e // 2 - steps[s // 2]) & (chips - 1)) + ((e + s) & 1)

    zs = nb // X_SIZE
    far_first = sorted(
        range(1, nb), key=lambda i: -(away(i // zs, X_SIZE) + away(i % zs, zs)))

    def bucket_peer(i):
        return ((b // zs + i // zs) & (X_SIZE - 1)) * zs + ((b + i) & (zs - 1))

    def signal(where):
        pl.semaphore_signal(barrier, inc=1, device_id=where, device_id_type=MESH)

    def send(src, dst, sems, where):
        return pltpu.make_async_remote_copy(
            src_ref=src, dst_ref=dst, send_sem=sems[0], recv_sem=sems[1],
            device_id=where, device_id_type=MESH)

    barrier = pltpu.get_barrier_semaphore()
    for s in reversed(range(1, ne)):
        signal({"entity": ahead(s)})
    loads = [
        pltpu.make_async_copy(src, dst, lsem.at[k])
        for k, (src, dst) in enumerate([
            (req_hbm, req_v), (table_hbm, table), (head_hbm, head_v), (tail_hbm, tail_v),
            (neg_hbm, neg_v), (rel_hbm, rel_v), (panel_hbm, panel),
        ])
    ]
    for load in loads:
        load.start()
    for i in far_first:
        signal({"bucket": bucket_peer(i)})

    loads[0].wait()
    req = req_v[...]
    repeat = (iota((cap, slots), 0) == lax.rem(iota((cap, slots), 1), cap)).astype(F32).astype(BF)
    high = mm((req >> 5).astype(F32).astype(BF), repeat)
    low = mm((req & 31).astype(F32).astype(BF), repeat)
    wide[...] = (high * 32.0 + low).astype(jnp.int32)
    for s in range(ne):
        mine = iota((1, slots), 1) // cap == s
        msg[s] = jnp.where(mine, wide[pl.ds(ahead(s), 1), :], 0)

    pl.semaphore_wait(barrier, ne + nb - 2)

    asks = {
        s: send(msg.at[s], reqbuf.at[s], (qs.at[s], qr.at[s]), {"entity": ahead(s)})
        for s in range(1, ne)
    }
    for s in reversed(range(1, ne)):
        asks[s].start()
    loads[1].wait()
    asked = msg[0]
    for s in range(1, ne):
        asks[s].wait()
        asked = asked + reqbuf[s]
    asked_all[0] = asked

    asked_col = to_col(asked.astype(F32)).astype(jnp.int32)
    pick = (iota((slots, table_rows), 1) == asked_col).astype(F32).astype(BF)
    rows[...] = mm(pick, table[...]).astype(BF)

    def at_slot(s):
        return slice(s * cap, (s + 1) * cap)

    def at_entity(o):
        return pl.ds(pl.multiple_of(o * cap, cap), cap)

    returns = {
        s: send(rows.at[at_slot(s)], fetched.at[at_entity(e)], (cs.at[s], cr.at[s]),
                {"entity": behind(s)})
        for s in range(1, ne)
    }
    for s in reversed(range(1, ne)):
        returns[s].start()
    lists = {
        i: send(asked_all.at[0], asked_all.at[i], (as_.at[i], ar.at[i]), {"bucket": bucket_peer(i)})
        for i in range(1, nb)
    }
    for i in far_first:
        lists[i].start()
    fetched[at_entity(e), :] = rows[at_slot(0), :]

    for load in loads[2:]:
        load.wait()
    tables = slot_tables(head_v, tail_v, neg_v, count_ref[0], slots)
    for s in range(1, ne):
        returns[s].wait()

    grad_proj, grad_rel = local_terms(fetched[...], panel[...], rel_v[...].astype(F32), tables)
    gf[...] = mm(grad_proj, panel[...]).astype(BF)

    grads = {
        s: send(gf.at[at_entity(ahead(s))], grecv.at[at_slot(s)], (es.at[s], er.at[s]),
                {"entity": ahead(s)})
        for s in range(1, ne)
    }
    for h in range(HALVES):
        for s in reversed(range(max(h * per_half, 1), (h + 1) * per_half)):
            grads[s].start()
    grecv[at_slot(0), :] = gf[at_entity(e), :]
    rel_out[...] = grad_rel
    proj_out[...] = grad_proj
    fetched_out[...] = fetched[...]

    def part(h, i):
        at = pl.ds(pl.multiple_of(bucket_peer(i) * width, width), width)
        return send(gt.at[h, at, :], frecv.at[h, i], (fs.at[h, i], fr.at[h, i]),
                    {"bucket": bucket_peer(i)})

    for h in range(HALVES):
        for s in range(max(h * per_half, 1), (h + 1) * per_half):
            grads[s].wait()
        piece = grecv[h * half_lanes : (h + 1) * half_lanes, :].astype(F32)
        gt[h] = piece.T.astype(BF)
        for i in far_first:
            part(h, i).start()
        frecv[h, 0] = gt[h, pl.ds(pl.multiple_of(b * width, width), width), :]
        if h == 0:
            for i in range(1, nb):
                lists[i].wait()
            for i in range(nb):
                for k in range(HALVES):
                    hi = asked_all[i, :, k * half_lanes : (k + 1) * half_lanes] & (LANES - 1)
                    hot[k, :, i * half_lanes : (i + 1) * half_lanes] = one_hot(hi, LANES).astype(BF)

    total = None
    for h in range(HALVES):
        for i in [0] + far_first[::-1]:
            if i:
                part(h, i).wait()
            lo = asked_all[i, :, h * half_lanes : (h + 1) * half_lanes] >> 7
            g = frecv[h, i].astype(F32)
            spread[h, :, i * half_lanes : (i + 1) * half_lanes] = jnp.concatenate(
                [jnp.where(lo == k, g, 0.0) for k in range(high_rows)], axis=0).astype(BF)
        share = mm_nt(spread[h], hot[h])
        total = share if total is None else total + share
    for k in range(high_rows):
        ent_ref[:, k * LANES : (k + 1) * LANES] = total[k * width : (k + 1) * width, :]


def finish(ent_ref, proj_ref, fetched_ref, rel_ref, ent_out, panel_out, rel_out, held, sem):
    outs = [
        pltpu.make_async_copy(ent_ref, ent_out, sem.at[0]),
        pltpu.make_async_copy(rel_ref, rel_out, sem.at[1]),
    ]
    for out in outs:
        out.start()
    half = held.shape[0] // 2
    for h in range(2):
        part = slice(h * half, (h + 1) * half)
        held[part, :] = mm_tn(proj_ref[:, part], fetched_ref[...])
        out = pltpu.make_async_copy(held.at[part], panel_out.at[part], sem.at[2 + h])
        out.start()
        outs.append(out)
    for out in outs:
        out.wait()


def body(ent_table, panels, rel_vecs, head_slots, tail_slots, negatives, requests, block_count):
    nb = lax.axis_size("bucket")
    ne = lax.axis_size("entity")
    rows, feat = ent_table.shape
    cap = requests.shape[2]
    slots = ne * cap
    width = feat // nb
    half = slots // HALVES
    vmem = pl.BlockSpec(memory_space=pltpu.VMEM)
    hbm = pl.BlockSpec(memory_space=pltpu.HBM)
    dma = pltpu.SemaphoreType.DMA
    shapes = (
        jax.ShapeDtypeStruct((width, rows), F32),
        jax.ShapeDtypeStruct((slots, feat), BF),
        jax.ShapeDtypeStruct((slots, feat), BF),
        jax.ShapeDtypeStruct((1, feat), F32),
    )
    ent_t, grad_proj, fetched, grad_rel = pl.pallas_call(
        functools.partial(kernel, nb, ne),
        out_shape=shapes,
        in_specs=[hbm] * 7 + [pl.BlockSpec(memory_space=pltpu.SMEM)],
        out_specs=(vmem,) * 4,
        scratch_shapes=[
            pltpu.VMEM((rows, feat), BF),
            pltpu.VMEM((feat, feat), BF),
            pltpu.VMEM(rel_vecs.shape, BF),
            pltpu.VMEM(head_slots.shape[1:], jnp.int32),
            pltpu.VMEM(tail_slots.shape[1:], jnp.int32),
            pltpu.VMEM(negatives.shape[1:], jnp.int32),
            pltpu.VMEM(requests.shape[1:], jnp.int32),
            pltpu.VMEM((ne, slots), jnp.int32),
            pltpu.VMEM((ne, 1, slots), jnp.int32),
            pltpu.VMEM((ne, 1, slots), jnp.int32),
            pltpu.VMEM((nb, 1, slots), jnp.int32),
            pltpu.VMEM((slots, feat), BF),
            pltpu.VMEM((slots, feat), BF),
            pltpu.VMEM((slots, feat), BF),
            pltpu.VMEM((slots, feat), BF),
            pltpu.VMEM((HALVES, feat, half), BF),
            pltpu.VMEM((HALVES, nb, width, half), BF),
            pltpu.VMEM((HALVES, rows // LANES * width, nb * half), BF),
            pltpu.VMEM((HALVES, LANES, nb * half), BF),
            dma((7,)),
            dma((ne,)), dma((ne,)),
            dma((nb,)), dma((nb,)),
            dma((ne,)), dma((ne,)),
            dma((ne,)), dma((ne,)),
            dma((HALVES, nb)), dma((HALVES, nb)),
        ],
        compiler_params=pltpu.CompilerParams(
            collective_id=0, has_side_effects=True, vmem_limit_bytes=40 * 1024 * 1024
        ),
        name="transr",
    )(
        *(pltpu.with_memory_space_constraint(x, pltpu.HBM) for x in (
            ent_table, panels[0], rel_vecs, head_slots[0], tail_slots[0], negatives[0],
            requests[0])),
        block_count,
    )
    ent_t, grad_panel, grad_rel = pl.pallas_call(
        finish,
        out_shape=(shapes[0], jax.ShapeDtypeStruct((feat, feat), F32), shapes[3]),
        in_specs=[vmem] * 4,
        out_specs=(hbm,) * 3,
        scratch_shapes=[pltpu.VMEM((feat, feat), F32), dma((4,))],
        compiler_params=pltpu.CompilerParams(vmem_limit_bytes=8 * 1024 * 1024),
        name="finish",
    )(ent_t, grad_proj, fetched, grad_rel)
    return (ent_t.T, grad_panel[None], grad_rel)


def solution(mesh):
    both = ("bucket", "entity")
    placed = (
        P("entity", None),
        P(both, None, None),
        P(both, None),
        P(both, None, None),
        P(both, None, None),
        P(both, None, None),
        P(both, None, None),
        P(both),
    )
    return jax.shard_map(
        body,
        mesh=mesh,
        in_specs=placed,
        out_specs=(P("entity", "bucket"), P(both, None, None), P(both, None)),
        check_vma=False,
    )
```

time: 61.5 us -> 52.7 us (0.86); the launches traced: 60.6 us -> 52.5 us
  local copies, waits for them, and re-layouts: 5.52 us -> 0 us
  Pallas kernels: 52.5 us -> 51.2 us
  matrix products: 1.29 us -> 0 us
    unnamed x16 -> x0, local copies, waits for them, and re-layouts: 5.52 us -> none
    dot_general x1 -> x0, matrix products: 1.29 us -> none  [body(): jnp.einsum('kd,ke->de', grad_proj, fetched, preferred_element_type=F32)]
    pallas_call x1 -> x2, Pallas kernels: 52.5 us -> 51.2 us  [the longest x1 50 us: body(): pl.pallas_call(functools.partial(kernel, nb, ne), out_shape=shapes, in_sp...]
where the time goes in v2:
time: 52.7 us; the launch traced here: 52.5 us
  Pallas kernels  51.2 us (97%)
  between operations  1.29 us (2%)
    pallas_call x1, Pallas kernels, body(): pl.pallas_call(functools.partial(kernel, nb, ne), out_shape=shapes, in_sp...  50 us
    pallas_call x1, Pallas kernels, body(): pl.pallas_call(finish, out_shape=(shapes[0], jax.ShapeDtypeStruct((feat,...  1.26 us

profile of v2, /device:TPU:6, one launch (start us, length us, event | category | flops | bytes accessed | tf_op | source)
XLA Modules:
  0.0 52.5 jit_solution(7319037434665348057)
XLA Ops:
  1.3 50.0 %transr.1 = (f32[16,1024]{1,0:T(8,128)S(1)}, bf16[256,512]{1,0:T(8,128)(2,1)S(1)}, bf16[256,512]{1,0:T(8,128)(2,1)S(1)}, f32[1,512]{1,0:T(1,128)S(1)}) custom-call(bf16[1024,512]{1,0:T(8,128)(2,1)} %table_hbm.1, bf16[512,512]{1,0:T(8,128)(2,1)} %bitcast.7, bf16[1,512]{1,0:T(2,128)(2,1)} %rel_hbm.1, s32[2,128]{1,0:T(2,128)} %bitcast.10, s32[2,128]{1,0:T(2,128)} %bitcast.11, ...), custom_call_target="tpu_custom_call" | custom-call | tf_op jit(solution)/shard_map/transr/pallas_call | solution.py:300
  51.3 1.3 %finish.1 = (f32[16,1024]{1,0:T(8,128)}, f32[512,512]{1,0:T(8,128)}, f32[1,512]{1,0:T(1,128)}) custom-call(f32[16,1024]{1,0:T(8,128)S(1)} %get-tuple-element.10.ent_ref, bf16[256,512]{1,0:T(8,128)(2,1)S(1)} %get-tuple-element.11.proj_ref, bf16[256,512]{1,0:T(8,128)(2,1)S(1)} %get-tuple-element.12.fetched_ref, f32[1,512]{1,0:T(1,128)S(1)} %get-tuple-element.13.rel_ref), custom_call_target="tpu_custom_call" | custom-call | tf_op jit(solution)/shard_map/finish/pallas_call | solution.py:342

commit v3 on v2

--- a/solution.py
+++ b/solution.py
@@ -10,6 +10,7 @@
 MARGIN = 2.0
 LANES = 128
 HALVES = 2
+GROUPS = 4
 X_SIZE = 4
 MESH = pl.DeviceIdType.MESH
 BF = jnp.bfloat16
@@ -103,7 +104,7 @@
     ent_ref, proj_out, fetched_out, rel_out,
     table, panel, rel_v, head_v, tail_v, neg_v, req_v, wide,
     msg, reqbuf, asked_all, rows, fetched, gf, grecv, gt, frecv, spread, hot,
-    lsem, qs, qr, as_, ar, cs, cr, es, er, fs, fr,
+    lsem, ask_sem, list_sem, row_sem, grad_sem, part_sem,
 ):
     b = lax.axis_index("bucket")
     e = lax.axis_index("entity")
@@ -134,10 +135,13 @@
     def signal(where):
         pl.semaphore_signal(barrier, inc=1, device_id=where, device_id_type=MESH)
 
-    def send(src, dst, sems, where):
+    def send(src, dst, sent, arrived, where):
         return pltpu.make_async_remote_copy(
-            src_ref=src, dst_ref=dst, send_sem=sems[0], recv_sem=sems[1],
+            src_ref=src, dst_ref=dst, send_sem=sent, recv_sem=arrived,
             device_id=where, device_id_type=MESH)
+
+    def whole(ref, sent, arrived, where):
+        return send(ref, ref, sent, arrived, where)
 
     barrier = pltpu.get_barrier_semaphore()
     for s in reversed(range(1, ne)):
@@ -166,16 +170,13 @@
 
     pl.semaphore_wait(barrier, ne + nb - 2)
 
-    asks = {
-        s: send(msg.at[s], reqbuf.at[s], (qs.at[s], qr.at[s]), {"entity": ahead(s)})
-        for s in range(1, ne)
-    }
     for s in reversed(range(1, ne)):
-        asks[s].start()
+        send(msg.at[s], reqbuf.at[s], ask_sem.at[0], ask_sem.at[1], {"entity": ahead(s)}).start()
     loads[1].wait()
+    asks = whole(reqbuf.at[1:ne], ask_sem.at[0], ask_sem.at[1], {"entity": ahead(1)})
+    asks.wait_recv()
     asked = msg[0]
     for s in range(1, ne):
-        asks[s].wait()
         asked = asked + reqbuf[s]
     asked_all[0] = asked
 
@@ -189,75 +190,77 @@
     def at_entity(o):
         return pl.ds(pl.multiple_of(o * cap, cap), cap)
 
-    returns = {
-        s: send(rows.at[at_slot(s)], fetched.at[at_entity(e)], (cs.at[s], cr.at[s]),
-                {"entity": behind(s)})
-        for s in range(1, ne)
-    }
     for s in reversed(range(1, ne)):
-        returns[s].start()
-    lists = {
-        i: send(asked_all.at[0], asked_all.at[i], (as_.at[i], ar.at[i]), {"bucket": bucket_peer(i)})
-        for i in range(1, nb)
-    }
+        send(rows.at[at_slot(s)], fetched.at[at_entity(e)], row_sem.at[0], row_sem.at[1],
+             {"entity": behind(s)}).start()
     for i in far_first:
-        lists[i].start()
+        send(asked_all.at[0], asked_all.at[i], list_sem.at[0], list_sem.at[1],
+             {"bucket": bucket_peer(i)}).start()
+    asks.wait_send()
     fetched[at_entity(e), :] = rows[at_slot(0), :]
 
     for load in loads[2:]:
         load.wait()
     tables = slot_tables(head_v, tail_v, neg_v, count_ref[0], slots)
-    for s in range(1, ne):
-        returns[s].wait()
+    returns = whole(rows.at[cap:], row_sem.at[0], row_sem.at[1], {"entity": ahead(1)})
+    returns.wait_recv()
 
     grad_proj, grad_rel = local_terms(fetched[...], panel[...], rel_v[...].astype(F32), tables)
     gf[...] = mm(grad_proj, panel[...]).astype(BF)
 
-    grads = {
-        s: send(gf.at[at_entity(ahead(s))], grecv.at[at_slot(s)], (es.at[s], er.at[s]),
-                {"entity": ahead(s)})
-        for s in range(1, ne)
-    }
     for h in range(HALVES):
         for s in reversed(range(max(h * per_half, 1), (h + 1) * per_half)):
-            grads[s].start()
+            send(gf.at[at_entity(ahead(s))], grecv.at[at_slot(s)], grad_sem.at[0],
+                 grad_sem.at[1 + h], {"entity": ahead(s)}).start()
     grecv[at_slot(0), :] = gf[at_entity(e), :]
     rel_out[...] = grad_rel
     proj_out[...] = grad_proj
     fetched_out[...] = fetched[...]
 
-    def part(h, i):
-        at = pl.ds(pl.multiple_of(bucket_peer(i) * width, width), width)
-        return send(gt.at[h, at, :], frecv.at[h, i], (fs.at[h, i], fr.at[h, i]),
-                    {"bucket": bucket_peer(i)})
-
+    returns.wait_send()
+
+    near_first = [0] + far_first[::-1]
+    group = nb // GROUPS
     for h in range(HALVES):
-        for s in range(max(h * per_half, 1), (h + 1) * per_half):
-            grads[s].wait()
-        piece = grecv[h * half_lanes : (h + 1) * half_lanes, :].astype(F32)
+        first = max(h * half_lanes, cap)
+        last = (h + 1) * half_lanes
+        whole(grecv.at[first:last], grad_sem.at[0], grad_sem.at[1 + h],
+              {"entity": ahead(1)}).wait_recv()
+        piece = grecv[h * half_lanes : last, :].astype(F32)
         gt[h] = piece.T.astype(BF)
-        for i in far_first:
-            part(h, i).start()
+        for p in reversed(range(1, nb)):
+            peer = bucket_peer(near_first[p])
+            send(gt.at[h, pl.ds(pl.multiple_of(peer * width, width), width), :],
+                 frecv.at[h, p], part_sem.at[0], part_sem.at[1 + h * GROUPS + p // group],
+                 {"bucket": peer}).start()
         frecv[h, 0] = gt[h, pl.ds(pl.multiple_of(b * width, width), width), :]
         if h == 0:
-            for i in range(1, nb):
-                lists[i].wait()
-            for i in range(nb):
+            lists = whole(asked_all.at[1:nb], list_sem.at[0], list_sem.at[1],
+                          {"bucket": bucket_peer(1)})
+            lists.wait()
+            for p in range(nb):
                 for k in range(HALVES):
-                    hi = asked_all[i, :, k * half_lanes : (k + 1) * half_lanes] & (LANES - 1)
-                    hot[k, :, i * half_lanes : (i + 1) * half_lanes] = one_hot(hi, LANES).astype(BF)
+                    hi = asked_all[near_first[p], :, k * half_lanes : (k + 1) * half_lanes]
+                    hot[k, :, p * half_lanes : (p + 1) * half_lanes] = one_hot(
+                        hi & (LANES - 1), LANES).astype(BF)
 
     total = None
     for h in range(HALVES):
-        for i in [0] + far_first[::-1]:
-            if i:
-                part(h, i).wait()
-            lo = asked_all[i, :, h * half_lanes : (h + 1) * half_lanes] >> 7
-            g = frecv[h, i].astype(F32)
-            spread[h, :, i * half_lanes : (i + 1) * half_lanes] = jnp.concatenate(
-                [jnp.where(lo == k, g, 0.0) for k in range(high_rows)], axis=0).astype(BF)
+        for q in range(GROUPS):
+            first = max(q * group, 1)
+            whole(frecv.at[h, first : (q + 1) * group], part_sem.at[0],
+                  part_sem.at[1 + h * GROUPS + q], {"bucket": bucket_peer(1)}).wait_recv()
+            for p in range(q * group, (q + 1) * group):
+                lo = asked_all[near_first[p], :, h * half_lanes : (h + 1) * half_lanes] >> 7
+                g = frecv[h, p].astype(F32)
+                spread[h, :, p * half_lanes : (p + 1) * half_lanes] = jnp.concatenate(
+                    [jnp.where(lo == k, g, 0.0) for k in range(high_rows)], axis=0).astype(BF)
         share = mm_nt(spread[h], hot[h])
         total = share if total is None else total + share
+    whole(grecv.at[cap:], grad_sem.at[0], grad_sem.at[1], {"entity": ahead(1)}).wait_send()
+    for h in range(HALVES):
+        whole(frecv.at[h, 1:nb], part_sem.at[0], part_sem.at[1],
+              {"bucket": bucket_peer(1)}).wait_send()
     for k in range(high_rows):
         ent_ref[:, k * LANES : (k + 1) * LANES] = total[k * width : (k + 1) * width, :]
 
@@ -323,11 +326,11 @@
             pltpu.VMEM((HALVES, rows // LANES * width, nb * half), BF),
             pltpu.VMEM((HALVES, LANES, nb * half), BF),
             dma((7,)),
-            dma((ne,)), dma((ne,)),
-            dma((nb,)), dma((nb,)),
-            dma((ne,)), dma((ne,)),
-            dma((ne,)), dma((ne,)),
-            dma((HALVES, nb)), dma((HALVES, nb)),
+            dma((2,)),
+            dma((2,)),
+            dma((2,)),
+            dma((1 + HALVES,)),
+            dma((1 + HALVES * GROUPS,)),
         ],
         compiler_params=pltpu.CompilerParams(
             collective_id=0, has_side_effects=True, vmem_limit_bytes=40 * 1024 * 1024

time: 52.7 us -> 49.3 us (0.935)
  Pallas kernels: 51.2 us -> 47.9 us
    pallas_call x1, Pallas kernels: 50 us -> 46.6 us  [body(): pl.pallas_call(functools.partial(kernel, nb, ne), out_shape=shapes, in_sp...]
where the time goes in v3:
time: 49.3 us; the launch traced here: 49.2 us
  Pallas kernels  47.9 us (97%)
  between operations  1.29 us (3%)
    pallas_call x1, Pallas kernels, body(): pl.pallas_call(functools.partial(kernel, nb, ne), out_shape=shapes, in_sp...  46.6 us
    pallas_call x1, Pallas kernels, body(): pl.pallas_call(finish, out_shape=(shapes[0], jax.ShapeDtypeStruct((feat,...  1.26 us

profile of v3, /device:TPU:6, one launch (start us, length us, event | category | flops | bytes accessed | tf_op | source)
XLA Modules:
  0.0 49.2 jit_solution(18280175302014562231)
XLA Ops:
  1.3 46.6 %transr.1 = (f32[16,1024]{1,0:T(8,128)S(1)}, bf16[256,512]{1,0:T(8,128)(2,1)S(1)}, bf16[256,512]{1,0:T(8,128)(2,1)S(1)}, f32[1,512]{1,0:T(1,128)S(1)}) custom-call(bf16[1024,512]{1,0:T(8,128)(2,1)} %table_hbm.1, bf16[512,512]{1,0:T(8,128)(2,1)} %bitcast.7, bf16[1,512]{1,0:T(2,128)(2,1)} %rel_hbm.1, s32[2,128]{1,0:T(2,128)} %bitcast.10, s32[2,128]{1,0:T(2,128)} %bitcast.11, ...), custom_call_target="tpu_custom_call" | custom-call | tf_op jit(solution)/shard_map/transr/pallas_call | solution.py:303
  47.9 1.3 %finish.1 = (f32[16,1024]{1,0:T(8,128)}, f32[512,512]{1,0:T(8,128)}, f32[1,512]{1,0:T(1,128)}) custom-call(f32[16,1024]{1,0:T(8,128)S(1)} %get-tuple-element.10.ent_ref, bf16[256,512]{1,0:T(8,128)(2,1)S(1)} %get-tuple-element.11.proj_ref, bf16[256,512]{1,0:T(8,128)(2,1)S(1)} %get-tuple-element.12.fetched_ref, f32[1,512]{1,0:T(1,128)S(1)} %get-tuple-element.13.rel_ref), custom_call_target="tpu_custom_call" | custom-call | tf_op jit(solution)/shard_map/finish/pallas_call | solution.py:345

commit v4 on v3

--- a/solution.py
+++ b/solution.py
@@ -101,7 +101,7 @@
 def kernel(
     nb, ne,
     table_hbm, panel_hbm, rel_hbm, head_hbm, tail_hbm, neg_hbm, req_hbm, count_ref,
-    ent_ref, proj_out, fetched_out, rel_out,
+    ent_ref, panel_out, rel_out,
     table, panel, rel_v, head_v, tail_v, neg_v, req_v, wide,
     msg, reqbuf, asked_all, rows, fetched, gf, grecv, gt, frecv, spread, hot,
     lsem, ask_sem, list_sem, row_sem, grad_sem, part_sem,
@@ -126,11 +126,20 @@
         return 2 * ((e // 2 - steps[s // 2]) & (chips - 1)) + ((e + s) & 1)
 
     zs = nb // X_SIZE
-    far_first = sorted(
-        range(1, nb), key=lambda i: -(away(i // zs, X_SIZE) + away(i % zs, zs)))
-
-    def bucket_peer(i):
-        return ((b // zs + i // zs) & (X_SIZE - 1)) * zs + ((b + i) & (zs - 1))
+    mine = lax.rem(b, zs) * X_SIZE + b // zs
+
+    def others(do):
+        def step(q, carry):
+            @pl.when(q != mine)
+            def _():
+                do({"bucket": lax.rem(q, X_SIZE) * zs + q // X_SIZE})
+
+            return carry
+
+        lax.fori_loop(0, nb, step, 0)
+
+    some_bucket = {"bucket": lax.rem(b + 1, nb)}
+    some_entity = {"entity": lax.rem(e + 1, ne)}
 
     def signal(where):
         pl.semaphore_signal(barrier, inc=1, device_id=where, device_id_type=MESH)
@@ -155,34 +164,23 @@
     ]
     for load in loads:
         load.start()
-    for i in far_first:
-        signal({"bucket": bucket_peer(i)})
+    others(signal)
 
     loads[0].wait()
     req = req_v[...]
-    repeat = (iota((cap, slots), 0) == lax.rem(iota((cap, slots), 1), cap)).astype(F32).astype(BF)
+    repeat = (iota((cap, half_lanes), 0) == lax.rem(iota((cap, half_lanes), 1), cap)).astype(F32).astype(BF)
     high = mm((req >> 5).astype(F32).astype(BF), repeat)
     low = mm((req & 31).astype(F32).astype(BF), repeat)
     wide[...] = (high * 32.0 + low).astype(jnp.int32)
     for s in range(ne):
-        mine = iota((1, slots), 1) // cap == s
-        msg[s] = jnp.where(mine, wide[pl.ds(ahead(s), 1), :], 0)
+        here = iota((1, half_lanes), 1) // cap == s % per_half
+        msg[s] = jnp.where(here, wide[pl.ds(ahead(s), 1), :], 0)
 
     pl.semaphore_wait(barrier, ne + nb - 2)
 
     for s in reversed(range(1, ne)):
-        send(msg.at[s], reqbuf.at[s], ask_sem.at[0], ask_sem.at[1], {"entity": ahead(s)}).start()
-    loads[1].wait()
-    asks = whole(reqbuf.at[1:ne], ask_sem.at[0], ask_sem.at[1], {"entity": ahead(1)})
-    asks.wait_recv()
-    asked = msg[0]
-    for s in range(1, ne):
-        asked = asked + reqbuf[s]
-    asked_all[0] = asked
-
-    asked_col = to_col(asked.astype(F32)).astype(jnp.int32)
-    pick = (iota((slots, table_rows), 1) == asked_col).astype(F32).astype(BF)
-    rows[...] = mm(pick, table[...]).astype(BF)
+        send(msg.at[s], reqbuf.at[s], ask_sem.at[0], ask_sem.at[1 + s // per_half],
+             {"entity": ahead(s)}).start()
 
     def at_slot(s):
         return slice(s * cap, (s + 1) * cap)
@@ -190,19 +188,30 @@
     def at_entity(o):
         return pl.ds(pl.multiple_of(o * cap, cap), cap)
 
-    for s in reversed(range(1, ne)):
-        send(rows.at[at_slot(s)], fetched.at[at_entity(e)], row_sem.at[0], row_sem.at[1],
-             {"entity": behind(s)}).start()
-    for i in far_first:
-        send(asked_all.at[0], asked_all.at[i], list_sem.at[0], list_sem.at[1],
-             {"bucket": bucket_peer(i)}).start()
-    asks.wait_send()
+    loads[1].wait()
+    for h in range(HALVES):
+        first = max(h * per_half, 1)
+        last = (h + 1) * per_half
+        whole(reqbuf.at[first:last], ask_sem.at[0], ask_sem.at[1 + h], some_entity).wait_recv()
+        asked = reqbuf[first] + (reqbuf[first + 1] if h else msg[0])
+        for s in range(first + 1 + h, last):
+            asked = asked + reqbuf[s]
+        asked_all[mine, :, h * half_lanes : last * cap] = asked
+        asked_col = to_col(asked.astype(F32)).astype(jnp.int32)
+        pick = (iota((half_lanes, table_rows), 1) == asked_col).astype(F32).astype(BF)
+        rows[h * half_lanes : last * cap, :] = mm(pick, table[...]).astype(BF)
+        for s in reversed(range(first, last)):
+            send(rows.at[at_slot(s)], fetched.at[at_entity(e)], row_sem.at[0], row_sem.at[1],
+                 {"entity": behind(s)}).start()
+    others(lambda peer: send(
+        asked_all.at[mine], asked_all.at[mine], list_sem.at[0], list_sem.at[1], peer).start())
+    whole(reqbuf.at[1:ne], ask_sem.at[0], ask_sem.at[1], some_entity).wait_send()
     fetched[at_entity(e), :] = rows[at_slot(0), :]
 
     for load in loads[2:]:
         load.wait()
     tables = slot_tables(head_v, tail_v, neg_v, count_ref[0], slots)
-    returns = whole(rows.at[cap:], row_sem.at[0], row_sem.at[1], {"entity": ahead(1)})
+    returns = whole(rows.at[cap:], row_sem.at[0], row_sem.at[1], some_entity)
     returns.wait_recv()
 
     grad_proj, grad_rel = local_terms(fetched[...], panel[...], rel_v[...].astype(F32), tables)
@@ -214,71 +223,64 @@
                  grad_sem.at[1 + h], {"entity": ahead(s)}).start()
     grecv[at_slot(0), :] = gf[at_entity(e), :]
     rel_out[...] = grad_rel
-    proj_out[...] = grad_proj
-    fetched_out[...] = fetched[...]
-
+    panel_out[...] = mm_tn(grad_proj, fetched[...])
     returns.wait_send()
 
-    near_first = [0] + far_first[::-1]
     group = nb // GROUPS
+    my_group = mine // group
+    my_columns = pl.ds(pl.multiple_of(b * width, width), width)
     for h in range(HALVES):
         first = max(h * half_lanes, cap)
         last = (h + 1) * half_lanes
-        whole(grecv.at[first:last], grad_sem.at[0], grad_sem.at[1 + h],
-              {"entity": ahead(1)}).wait_recv()
-        piece = grecv[h * half_lanes : last, :].astype(F32)
-        gt[h] = piece.T.astype(BF)
-        for p in reversed(range(1, nb)):
-            peer = bucket_peer(near_first[p])
-            send(gt.at[h, pl.ds(pl.multiple_of(peer * width, width), width), :],
-                 frecv.at[h, p], part_sem.at[0], part_sem.at[1 + h * GROUPS + p // group],
-                 {"bucket": peer}).start()
-        frecv[h, 0] = gt[h, pl.ds(pl.multiple_of(b * width, width), width), :]
+        whole(grecv.at[first:last], grad_sem.at[0], grad_sem.at[1 + h], some_entity).wait_recv()
+        gt[h] = grecv[h * half_lanes : last, :].astype(F32).T.astype(BF)
+
+        def part(peer, h=h):
+            columns = pl.ds(pl.multiple_of(peer["bucket"] * width, width), width)
+            send(gt.at[h, columns, :], frecv.at[h, mine], part_sem.at[0],
+                 part_sem.at[1 + h * GROUPS + my_group], peer).start()
+
+        others(part)
+        frecv[h, mine] = gt[h, my_columns, :]
         if h == 0:
-            lists = whole(asked_all.at[1:nb], list_sem.at[0], list_sem.at[1],
-                          {"bucket": bucket_peer(1)})
-            lists.wait()
-            for p in range(nb):
+            whole(asked_all.at[1:nb], list_sem.at[0], list_sem.at[1], some_bucket).wait()
+            for q in range(nb):
                 for k in range(HALVES):
-                    hi = asked_all[near_first[p], :, k * half_lanes : (k + 1) * half_lanes]
-                    hot[k, :, p * half_lanes : (p + 1) * half_lanes] = one_hot(
-                        hi & (LANES - 1), LANES).astype(BF)
+                    hi = asked_all[q, :, k * half_lanes : (k + 1) * half_lanes] & (LANES - 1)
+                    hot[k, :, q * half_lanes : (q + 1) * half_lanes] = one_hot(hi, LANES).astype(BF)
 
     total = None
     for h in range(HALVES):
-        for q in range(GROUPS):
-            first = max(q * group, 1)
-            whole(frecv.at[h, first : (q + 1) * group], part_sem.at[0],
-                  part_sem.at[1 + h * GROUPS + q], {"bucket": bucket_peer(1)}).wait_recv()
-            for p in range(q * group, (q + 1) * group):
-                lo = asked_all[near_first[p], :, h * half_lanes : (h + 1) * half_lanes] >> 7
-                g = frecv[h, p].astype(F32)
-                spread[h, :, p * half_lanes : (p + 1) * half_lanes] = jnp.concatenate(
-                    [jnp.where(lo == k, g, 0.0) for k in range(high_rows)], axis=0).astype(BF)
-        share = mm_nt(spread[h], hot[h])
-        total = share if total is None else total + share
-    whole(grecv.at[cap:], grad_sem.at[0], grad_sem.at[1], {"entity": ahead(1)}).wait_send()
-    for h in range(HALVES):
-        whole(frecv.at[h, 1:nb], part_sem.at[0], part_sem.at[1],
-              {"bucket": bucket_peer(1)}).wait_send()
+        for k in range(GROUPS):
+            def arrived(count, h=h, k=k):
+                whole(frecv.at[h, k * group : k * group + count], part_sem.at[0],
+                      part_sem.at[1 + h * GROUPS + k], some_bucket).wait_recv()
+
+            pl.when(my_group == k)(lambda: arrived(group - 1))
+            pl.when(my_group != k)(lambda: arrived(group))
+            lanes = slice(k * group * half_lanes, (k + 1) * group * half_lanes)
+            for q in range(k * group, (k + 1) * group):
+                lo = asked_all[q, :, h * half_lanes : (h + 1) * half_lanes] >> 7
+                g = frecv[h, q].astype(F32)
+                spread[h, :, q * half_lanes : (q + 1) * half_lanes] = jnp.concatenate(
+                    [jnp.where(lo == r, g, 0.0) for r in range(high_rows)], axis=0).astype(BF)
+            share = mm_nt(spread[h, :, lanes], hot[h, :, lanes])
+            total = share if total is None else total + share
+    whole(grecv.at[cap:], grad_sem.at[0], grad_sem.at[1], some_entity).wait_send()
+    for h in range(HALVES):
+        whole(frecv.at[h, 1:nb], part_sem.at[0], part_sem.at[1], some_bucket).wait_send()
     for k in range(high_rows):
         ent_ref[:, k * LANES : (k + 1) * LANES] = total[k * width : (k + 1) * width, :]
 
 
-def finish(ent_ref, proj_ref, fetched_ref, rel_ref, ent_out, panel_out, rel_out, held, sem):
+def finish(ent_ref, panel_ref, rel_ref, ent_out, panel_out, rel_out, sem):
     outs = [
-        pltpu.make_async_copy(ent_ref, ent_out, sem.at[0]),
-        pltpu.make_async_copy(rel_ref, rel_out, sem.at[1]),
+        pltpu.make_async_copy(src, dst, sem.at[k])
+        for k, (src, dst) in enumerate([
+            (panel_ref, panel_out), (ent_ref, ent_out), (rel_ref, rel_out)])
     ]
     for out in outs:
         out.start()
-    half = held.shape[0] // 2
-    for h in range(2):
-        part = slice(h * half, (h + 1) * half)
-        held[part, :] = mm_tn(proj_ref[:, part], fetched_ref[...])
-        out = pltpu.make_async_copy(held.at[part], panel_out.at[part], sem.at[2 + h])
-        out.start()
-        outs.append(out)
     for out in outs:
         out.wait()
 
@@ -296,15 +298,14 @@
     dma = pltpu.SemaphoreType.DMA
     shapes = (
         jax.ShapeDtypeStruct((width, rows), F32),
-        jax.ShapeDtypeStruct((slots, feat), BF),
-        jax.ShapeDtypeStruct((slots, feat), BF),
+        jax.ShapeDtypeStruct((feat, feat), F32),
         jax.ShapeDtypeStruct((1, feat), F32),
     )
-    ent_t, grad_proj, fetched, grad_rel = pl.pallas_call(
+    results = pl.pallas_call(
         functools.partial(kernel, nb, ne),
         out_shape=shapes,
         in_specs=[hbm] * 7 + [pl.BlockSpec(memory_space=pltpu.SMEM)],
-        out_specs=(vmem,) * 4,
+        out_specs=(vmem,) * 3,
         scratch_shapes=[
             pltpu.VMEM((rows, feat), BF),
             pltpu.VMEM((feat, feat), BF),
@@ -313,9 +314,9 @@
             pltpu.VMEM(tail_slots.shape[1:], jnp.int32),
             pltpu.VMEM(negatives.shape[1:], jnp.int32),
             pltpu.VMEM(requests.shape[1:], jnp.int32),
-            pltpu.VMEM((ne, slots), jnp.int32),
-            pltpu.VMEM((ne, 1, slots), jnp.int32),
-            pltpu.VMEM((ne, 1, slots), jnp.int32),
+            pltpu.VMEM((ne, half), jnp.int32),
+            pltpu.VMEM((ne, 1, half), jnp.int32),
+            pltpu.VMEM((ne, 1, half), jnp.int32),
             pltpu.VMEM((nb, 1, slots), jnp.int32),
             pltpu.VMEM((slots, feat), BF),
             pltpu.VMEM((slots, feat), BF),
@@ -326,7 +327,7 @@
             pltpu.VMEM((HALVES, rows // LANES * width, nb * half), BF),
             pltpu.VMEM((HALVES, LANES, nb * half), BF),
             dma((7,)),
-            dma((2,)),
+            dma((1 + HALVES,)),
             dma((2,)),
             dma((2,)),
             dma((1 + HALVES,)),
@@ -344,13 +345,13 @@
     )
     ent_t, grad_panel, grad_rel = pl.pallas_call(
         finish,
-        out_shape=(shapes[0], jax.ShapeDtypeStruct((feat, feat), F32), shapes[3]),
-        in_specs=[vmem] * 4,
+        out_shape=shapes,
+        in_specs=[vmem] * 3,
         out_specs=(hbm,) * 3,
-        scratch_shapes=[pltpu.VMEM((feat, feat), F32), dma((4,))],
+        scratch_shapes=[dma((3,))],
         compiler_params=pltpu.CompilerParams(vmem_limit_bytes=8 * 1024 * 1024),
         name="finish",
-    )(ent_t, grad_proj, fetched, grad_rel)
+    )(*results)
     return (ent_t.T, grad_panel[None], grad_rel)
 
 

time: 49.3 us -> 46.8 us (0.949)
  Pallas kernels: 47.9 us -> 45.2 us
    pallas_call x1, Pallas kernels: 46.6 us -> 44.2 us  [body(): pl.pallas_call(functools.partial(kernel, nb, ne), out_shape=shapes, in_sp...]
where the time goes in v4:
time: 46.8 us; the launch traced here: 46.5 us
  Pallas kernels  45.2 us (97%)
  between operations  1.29 us (3%)
    pallas_call x1, Pallas kernels, body(): pl.pallas_call(functools.partial(kernel, nb, ne), out_shape=shapes, in_sp...  44.2 us
    pallas_call x1, Pallas kernels, body(): pl.pallas_call(finish, out_shape=shapes, in_specs=[vmem] * 3, out_specs=(...  1.01 us

profile of v4, /device:TPU:6, one launch (start us, length us, event | category | flops | bytes accessed | tf_op | source)
XLA Modules:
  0.0 46.5 jit_solution(15701208046506800110)
XLA Ops:
  1.3 44.2 %transr.1 = (f32[16,1024]{1,0:T(8,128)S(1)}, f32[512,512]{1,0:T(8,128)S(1)}, f32[1,512]{1,0:T(1,128)S(1)}) custom-call(bf16[1024,512]{1,0:T(8,128)(2,1)} %table_hbm.1, bf16[512,512]{1,0:T(8,128)(2,1)} %bitcast.7, bf16[1,512]{1,0:T(2,128)(2,1)} %rel_hbm.1, s32[2,128]{1,0:T(2,128)} %bitcast.10, s32[2,128]{1,0:T(2,128)} %bitcast.11, s32[2,512]{1,0:T(2,128)} %bitcast.9, ...), custom_call_target="tpu_custom_call" | custom-call | tf_op jit(solution)/shard_map/transr/pallas_call | solution.py:304
  45.5 1.0 %finish.1 = (f32[16,1024]{1,0:T(8,128)}, f32[512,512]{1,0:T(8,128)}, f32[1,512]{1,0:T(1,128)}) custom-call(f32[16,1024]{1,0:T(8,128)S(1)} %get-tuple-element.9.ent_ref, f32[512,512]{1,0:T(8,128)S(1)} %get-tuple-element.10.panel_ref, f32[1,512]{1,0:T(1,128)S(1)} %get-tuple-element.11.rel_ref), custom_call_target="tpu_custom_call" | custom-call | tf_op jit(solution)/shard_map/finish/pallas_call | solution.py:346

commit v5 on v4

--- a/solution.py
+++ b/solution.py
@@ -11,6 +11,7 @@
 LANES = 128
 HALVES = 2
 GROUPS = 4
+CUTS = (0, 2, 8)
 X_SIZE = 4
 MESH = pl.DeviceIdType.MESH
 BF = jnp.bfloat16
@@ -102,7 +103,7 @@
     nb, ne,
     table_hbm, panel_hbm, rel_hbm, head_hbm, tail_hbm, neg_hbm, req_hbm, count_ref,
     ent_ref, panel_out, rel_out,
-    table, panel, rel_v, head_v, tail_v, neg_v, req_v, wide,
+    table, panel, panel_q, rel_v, head_v, tail_v, neg_v, req_v, wide,
     msg, reqbuf, asked_all, rows, fetched, gf, grecv, gt, frecv, spread, hot,
     lsem, ask_sem, list_sem, row_sem, grad_sem, part_sem,
 ):
@@ -128,15 +129,15 @@
     zs = nb // X_SIZE
     mine = lax.rem(b, zs) * X_SIZE + b // zs
 
+    far_first = sorted(
+        range(1, nb), key=lambda i: -(away(i // zs, X_SIZE) + away(i % zs, zs)))
+
+    def bucket_peer(i):
+        return ((b // zs + i // zs) & (X_SIZE - 1)) * zs + ((b + i) & (zs - 1))
+
     def others(do):
-        def step(q, carry):
-            @pl.when(q != mine)
-            def _():
-                do({"bucket": lax.rem(q, X_SIZE) * zs + q // X_SIZE})
-
-            return carry
-
-        lax.fori_loop(0, nb, step, 0)
+        for q in range(nb):
+            pl.when(q != mine)(functools.partial(do, q % X_SIZE * zs + q // X_SIZE))
 
     some_bucket = {"bucket": lax.rem(b + 1, nb)}
     some_entity = {"entity": lax.rem(e + 1, ne)}
@@ -152,9 +153,6 @@
     def whole(ref, sent, arrived, where):
         return send(ref, ref, sent, arrived, where)
 
-    barrier = pltpu.get_barrier_semaphore()
-    for s in reversed(range(1, ne)):
-        signal({"entity": ahead(s)})
     loads = [
         pltpu.make_async_copy(src, dst, lsem.at[k])
         for k, (src, dst) in enumerate([
@@ -162,9 +160,14 @@
             (neg_hbm, neg_v), (rel_hbm, rel_v), (panel_hbm, panel),
         ])
     ]
-    for load in loads:
+    barrier = pltpu.get_barrier_semaphore()
+    loads[0].start()
+    for i in far_first:
+        signal({"bucket": bucket_peer(i)})
+    for s in reversed(range(1, ne)):
+        signal({"entity": ahead(s)})
+    for load in loads[1:]:
         load.start()
-    others(signal)
 
     loads[0].wait()
     req = req_v[...]
@@ -204,23 +207,32 @@
             send(rows.at[at_slot(s)], fetched.at[at_entity(e)], row_sem.at[0], row_sem.at[1],
                  {"entity": behind(s)}).start()
     others(lambda peer: send(
-        asked_all.at[mine], asked_all.at[mine], list_sem.at[0], list_sem.at[1], peer).start())
+        asked_all.at[mine], asked_all.at[mine], list_sem.at[0], list_sem.at[1],
+        {"bucket": peer}).start())
     whole(reqbuf.at[1:ne], ask_sem.at[0], ask_sem.at[1], some_entity).wait_send()
     fetched[at_entity(e), :] = rows[at_slot(0), :]
 
     for load in loads[2:]:
         load.wait()
+    feat = panel.shape[1]
+    at = iota((feat, feat), 1)
+    q_of = at // width
+    source = (lax.rem(q_of, X_SIZE) * zs + q_of // X_SIZE) * width + lax.rem(at, width)
+    order = (iota((feat, feat), 0) == source).astype(F32).astype(BF)
+    panel_q[...] = mm(panel[...], order).astype(BF)
     tables = slot_tables(head_v, tail_v, neg_v, count_ref[0], slots)
     returns = whole(rows.at[cap:], row_sem.at[0], row_sem.at[1], some_entity)
     returns.wait_recv()
 
     grad_proj, grad_rel = local_terms(fetched[...], panel[...], rel_v[...].astype(F32), tables)
-    gf[...] = mm(grad_proj, panel[...]).astype(BF)
-
-    for h in range(HALVES):
+    gf[...] = mm(grad_proj, panel_q[...]).astype(BF)
+
+    pieces = [(cut, h) for cut in zip(CUTS, CUTS[1:]) for h in range(HALVES)]
+    for n, (cut, h) in enumerate(pieces):
+        columns = slice(cut[0] * nb // 8 * width, cut[1] * nb // 8 * width)
         for s in reversed(range(max(h * per_half, 1), (h + 1) * per_half)):
-            send(gf.at[at_entity(ahead(s))], grecv.at[at_slot(s)], grad_sem.at[0],
-                 grad_sem.at[1 + h], {"entity": ahead(s)}).start()
+            send(gf.at[at_entity(ahead(s)), columns], grecv.at[at_slot(s), columns],
+                 grad_sem.at[0], grad_sem.at[1 + n], {"entity": ahead(s)}).start()
     grecv[at_slot(0), :] = gf[at_entity(e), :]
     rel_out[...] = grad_rel
     panel_out[...] = mm_tn(grad_proj, fetched[...])
@@ -228,21 +240,24 @@
 
     group = nb // GROUPS
     my_group = mine // group
-    my_columns = pl.ds(pl.multiple_of(b * width, width), width)
-    for h in range(HALVES):
+    my_columns = pl.ds(pl.multiple_of(mine * width, width), width)
+    def part(h, q):
+        peer = q % X_SIZE * zs + q // X_SIZE
+        send(gt.at[h, q * width : (q + 1) * width, :], frecv.at[h, mine], part_sem.at[0],
+             part_sem.at[1 + h * GROUPS + my_group], {"bucket": peer}).start()
+
+    for n, (cut, h) in enumerate(pieces):
+        columns = slice(cut[0] * nb // 8 * width, cut[1] * nb // 8 * width)
         first = max(h * half_lanes, cap)
         last = (h + 1) * half_lanes
-        whole(grecv.at[first:last], grad_sem.at[0], grad_sem.at[1 + h], some_entity).wait_recv()
-        gt[h] = grecv[h * half_lanes : last, :].astype(F32).T.astype(BF)
-
-        def part(peer, h=h):
-            columns = pl.ds(pl.multiple_of(peer["bucket"] * width, width), width)
-            send(gt.at[h, columns, :], frecv.at[h, mine], part_sem.at[0],
-                 part_sem.at[1 + h * GROUPS + my_group], peer).start()
-
-        others(part)
-        frecv[h, mine] = gt[h, my_columns, :]
-        if h == 0:
+        whole(grecv.at[first:last, columns], grad_sem.at[0], grad_sem.at[1 + n],
+              some_entity).wait_recv()
+        gt[h, columns, :] = grecv[h * half_lanes : last, columns].astype(F32).T.astype(BF)
+        for q in range(cut[0] * nb // 8, cut[1] * nb // 8):
+            pl.when(q != mine)(functools.partial(part, h, q))
+        if cut[1] == CUTS[-1]:
+            frecv[h, mine] = gt[h, my_columns, :]
+        if n == 0:
             whole(asked_all.at[1:nb], list_sem.at[0], list_sem.at[1], some_bucket).wait()
             for q in range(nb):
                 for k in range(HALVES):
@@ -308,6 +323,7 @@
         out_specs=(vmem,) * 3,
         scratch_shapes=[
             pltpu.VMEM((rows, feat), BF),
+            pltpu.VMEM((feat, feat), BF),
             pltpu.VMEM((feat, feat), BF),
             pltpu.VMEM(rel_vecs.shape, BF),
             pltpu.VMEM(head_slots.shape[1:], jnp.int32),
@@ -330,7 +346,7 @@
             dma((1 + HALVES,)),
             dma((2,)),
             dma((2,)),
-            dma((1 + HALVES,)),
+            dma((1 + HALVES * (len(CUTS) - 1),)),
             dma((1 + HALVES * GROUPS,)),
         ],
         compiler_params=pltpu.CompilerParams(

time: 46.8 us -> 43.8 us (0.936)
  Pallas kernels: 45.2 us -> 42.4 us
    pallas_call x1, Pallas kernels: 44.2 us -> 41.4 us  [body(): pl.pallas_call(functools.partial(kernel, nb, ne), out_shape=shapes, in_sp...]
where the time goes in v5:
time: 43.8 us; the launch traced here: 43.7 us
  Pallas kernels  42.4 us (97%)
  between operations  1.29 us (3%)
    pallas_call x1, Pallas kernels, body(): pl.pallas_call(functools.partial(kernel, nb, ne), out_shape=shapes, in_sp...  41.4 us
    pallas_call x1, Pallas kernels, body(): pl.pallas_call(finish, out_shape=shapes, in_specs=[vmem] * 3, out_specs=(...  1.01 us

profile of v5, /device:TPU:6, one launch (start us, length us, event | category | flops | bytes accessed | tf_op | source)
XLA Modules:
  0.0 43.7 jit_solution(6194791732754305574)
XLA Ops:
  1.3 41.4 %transr.1 = (f32[16,1024]{1,0:T(8,128)S(1)}, f32[512,512]{1,0:T(8,128)S(1)}, f32[1,512]{1,0:T(1,128)S(1)}) custom-call(bf16[1024,512]{1,0:T(8,128)(2,1)} %table_hbm.1, bf16[512,512]{1,0:T(8,128)(2,1)} %bitcast.7, bf16[1,512]{1,0:T(2,128)(2,1)} %rel_hbm.1, s32[2,128]{1,0:T(2,128)} %bitcast.10, s32[2,128]{1,0:T(2,128)} %bitcast.11, s32[2,512]{1,0:T(2,128)} %bitcast.9, ...), custom_call_target="tpu_custom_call" | custom-call | tf_op jit(solution)/shard_map/transr/pallas_call | solution.py:319
  42.6 1.0 %finish.1 = (f32[16,1024]{1,0:T(8,128)}, f32[512,512]{1,0:T(8,128)}, f32[1,512]{1,0:T(1,128)}) custom-call(f32[16,1024]{1,0:T(8,128)S(1)} %get-tuple-element.9.ent_ref, f32[512,512]{1,0:T(8,128)S(1)} %get-tuple-element.10.panel_ref, f32[1,512]{1,0:T(1,128)S(1)} %get-tuple-element.11.rel_ref), custom_call_target="tpu_custom_call" | custom-call | tf_op jit(solution)/shard_map/finish/pallas_call | solution.py:362

commit v6 on v5

--- a/solution.py
+++ b/solution.py
@@ -64,16 +64,19 @@
         hits = jnp.sum(one_hot(neg_ref[j : j + 1, :], slots), axis=1, keepdims=True)
         count = jnp.where(block_of == j, to_row(hits), count)
     count = count * (live * (1.0 / neg_ref.shape[1]))
-    return head_t.astype(BF), tail_t.astype(BF), head_t.T.astype(BF), tail_t.T.astype(BF), live, count
+    ends_t = jnp.concatenate([head_t, tail_t], axis=1)
+    return ends_t.astype(BF), ends_t.T.astype(BF), live, count
 
 
 def local_terms(fetched, panel, rel, tables):
-    head_t, tail_t, head, tail, live, count = tables
+    ends_t, ends, live, count = tables
+    edges = live.shape[0]
     proj = mm_nt(fetched, panel).astype(BF)
     proj_f = proj.astype(F32)
-    centers = (mm(head, proj) + rel).astype(BF)
+    found = mm(ends, proj)
+    centers = (found[:edges] + rel).astype(BF)
     center_f = centers.astype(F32)
-    offset = center_f - mm(tail, proj)
+    offset = center_f - found[edges:]
     pos_weight = jax.nn.sigmoid(jnp.sum(offset * offset, axis=1, keepdims=True) - MARGIN) * live
     proj_sq = to_row(jnp.sum(proj_f * proj_f, axis=1, keepdims=True))
     center_sq = jnp.sum(center_f * center_f, axis=1, keepdims=True)
@@ -86,13 +89,10 @@
         + 2.0 * jnp.sum(weight, axis=1, keepdims=True) * center_f
         - 2.0 * mm(weight.astype(BF), proj)
     )
-    grad_proj = (
-        mm(head_t, grad_center.astype(BF))
-        - mm(tail_t, pulled.astype(BF))
-        + 2.0 * jnp.sum(weight_t, axis=1, keepdims=True) * proj_f
-        - 2.0 * mm(weight_t.astype(BF), centers)
-    ).astype(BF)
-    return grad_proj, jnp.sum(grad_center, axis=0, keepdims=True)
+    onto = jnp.concatenate([ends_t, (-2.0 * weight_t).astype(BF)], axis=1)
+    terms = jnp.concatenate([grad_center.astype(BF), (-pulled).astype(BF), centers], axis=0)
+    grad_proj = mm(onto, terms) + 2.0 * jnp.sum(weight_t, axis=1, keepdims=True) * proj_f
+    return grad_proj.astype(BF), jnp.sum(grad_center, axis=0, keepdims=True)
 
 
 def away(step, size):
@@ -225,17 +225,17 @@
     returns.wait_recv()
 
     grad_proj, grad_rel = local_terms(fetched[...], panel[...], rel_v[...].astype(F32), tables)
-    gf[...] = mm(grad_proj, panel_q[...]).astype(BF)
 
     pieces = [(cut, h) for cut in zip(CUTS, CUTS[1:]) for h in range(HALVES)]
     for n, (cut, h) in enumerate(pieces):
         columns = slice(cut[0] * nb // 8 * width, cut[1] * nb // 8 * width)
+        if h == 0:
+            gf[:, columns] = mm(grad_proj, panel_q[:, columns]).astype(BF)
         for s in reversed(range(max(h * per_half, 1), (h + 1) * per_half)):
             send(gf.at[at_entity(ahead(s)), columns], grecv.at[at_slot(s), columns],
                  grad_sem.at[0], grad_sem.at[1 + n], {"entity": ahead(s)}).start()
     grecv[at_slot(0), :] = gf[at_entity(e), :]
     rel_out[...] = grad_rel
-    panel_out[...] = mm_tn(grad_proj, fetched[...])
     returns.wait_send()
 
     group = nb // GROUPS
@@ -257,12 +257,13 @@
             pl.when(q != mine)(functools.partial(part, h, q))
         if cut[1] == CUTS[-1]:
             frecv[h, mine] = gt[h, my_columns, :]
-        if n == 0:
-            whole(asked_all.at[1:nb], list_sem.at[0], list_sem.at[1], some_bucket).wait()
-            for q in range(nb):
-                for k in range(HALVES):
-                    hi = asked_all[q, :, k * half_lanes : (k + 1) * half_lanes] & (LANES - 1)
-                    hot[k, :, q * half_lanes : (q + 1) * half_lanes] = one_hot(hi, LANES).astype(BF)
+
+    panel_out[...] = mm_tn(grad_proj, fetched[...])
+    whole(asked_all.at[1:nb], list_sem.at[0], list_sem.at[1], some_bucket).wait()
+    for q in range(nb):
+        for k in range(HALVES):
+            hi = asked_all[q, :, k * half_lanes : (k + 1) * half_lanes] & (LANES - 1)
+            hot[k, :, q * half_lanes : (q + 1) * half_lanes] = one_hot(hi, LANES).astype(BF)
 
     total = None
     for h in range(HALVES):

time: 43.8 us -> 43.8 us (level)
  no operation moved by 1% of the time
where the time goes in v6:
time: 43.8 us; the launch traced here: 43.6 us
  Pallas kernels  42.3 us (97%)
  between operations  1.29 us (3%)
    pallas_call x1, Pallas kernels, body(): pl.pallas_call(functools.partial(kernel, nb, ne), out_shape=shapes, in_sp...  41.3 us
    pallas_call x1, Pallas kernels, body(): pl.pallas_call(finish, out_shape=shapes, in_specs=[vmem] * 3, out_specs=(...  1.01 us

profile of v6, /device:TPU:6, one launch (start us, length us, event | category | flops | bytes accessed | tf_op | source)
XLA Modules:
  0.0 43.6 jit_solution(717075299762639234)
XLA Ops:
  1.3 41.3 %transr.1 = (f32[16,1024]{1,0:T(8,128)S(1)}, f32[512,512]{1,0:T(8,128)S(1)}, f32[1,512]{1,0:T(1,128)S(1)}) custom-call(bf16[1024,512]{1,0:T(8,128)(2,1)} %table_hbm.1, bf16[512,512]{1,0:T(8,128)(2,1)} %bitcast.7, bf16[1,512]{1,0:T(2,128)(2,1)} %rel_hbm.1, s32[2,128]{1,0:T(2,128)} %bitcast.10, s32[2,128]{1,0:T(2,128)} %bitcast.11, s32[2,512]{1,0:T(2,128)} %bitcast.9, ...), custom_call_target="tpu_custom_call" | custom-call | tf_op jit(solution)/shard_map/transr/pallas_call | solution.py:320
  42.6 1.0 %finish.1 = (f32[16,1024]{1,0:T(8,128)}, f32[512,512]{1,0:T(8,128)}, f32[1,512]{1,0:T(1,128)}) custom-call(f32[16,1024]{1,0:T(8,128)S(1)} %get-tuple-element.9.ent_ref, f32[512,512]{1,0:T(8,128)S(1)} %get-tuple-element.10.panel_ref, f32[1,512]{1,0:T(1,128)S(1)} %get-tuple-element.11.rel_ref), custom_call_target="tpu_custom_call" | custom-call | tf_op jit(solution)/shard_map/finish/pallas_call | solution.py:363

commit v7 on v5

--- a/solution.py
+++ b/solution.py
@@ -252,7 +252,7 @@
         last = (h + 1) * half_lanes
         whole(grecv.at[first:last, columns], grad_sem.at[0], grad_sem.at[1 + n],
               some_entity).wait_recv()
-        gt[h, columns, :] = grecv[h * half_lanes : last, columns].astype(F32).T.astype(BF)
+        gt[h, columns, :] = grecv[h * half_lanes : last, columns].T
         for q in range(cut[0] * nb // 8, cut[1] * nb // 8):
             pl.when(q != mine)(functools.partial(part, h, q))
         if cut[1] == CUTS[-1]:

time: 43.8 us -> 43.7 us (level)
  no operation moved by 1% of the time
where the time goes in v7:
time: 43.7 us; the launch traced here: 43.6 us
  Pallas kernels  42.3 us (97%)
  between operations  1.29 us (3%)
    pallas_call x1, Pallas kernels, body(): pl.pallas_call(functools.partial(kernel, nb, ne), out_shape=shapes, in_sp...  41.3 us
    pallas_call x1, Pallas kernels, body(): pl.pallas_call(finish, out_shape=shapes, in_specs=[vmem] * 3, out_specs=(...  1.01 us

profile of v7, /device:TPU:6, one launch (start us, length us, event | category | flops | bytes accessed | tf_op | source)
XLA Modules:
  0.0 43.6 jit_solution(1299744094869027361)
XLA Ops:
  1.3 41.3 %transr.1 = (f32[16,1024]{1,0:T(8,128)S(1)}, f32[512,512]{1,0:T(8,128)S(1)}, f32[1,512]{1,0:T(1,128)S(1)}) custom-call(bf16[1024,512]{1,0:T(8,128)(2,1)} %table_hbm.1, bf16[512,512]{1,0:T(8,128)(2,1)} %bitcast.7, bf16[1,512]{1,0:T(2,128)(2,1)} %rel_hbm.1, s32[2,128]{1,0:T(2,128)} %bitcast.10, s32[2,128]{1,0:T(2,128)} %bitcast.11, s32[2,512]{1,0:T(2,128)} %bitcast.9, ...), custom_call_target="tpu_custom_call" | custom-call | tf_op jit(solution)/shard_map/transr/pallas_call | solution.py:319
  42.6 1.0 %finish.1 = (f32[16,1024]{1,0:T(8,128)}, f32[512,512]{1,0:T(8,128)}, f32[1,512]{1,0:T(1,128)}) custom-call(f32[16,1024]{1,0:T(8,128)S(1)} %get-tuple-element.9.ent_ref, f32[512,512]{1,0:T(8,128)S(1)} %get-tuple-element.10.panel_ref, f32[1,512]{1,0:T(1,128)S(1)} %get-tuple-element.11.rel_ref), custom_call_target="tpu_custom_call" | custom-call | tf_op jit(solution)/shard_map/finish/pallas_call | solution.py:362
